TPU v7x, 256 devices: a whole 4x4x8 slice. The times are simulated.
256 devices in a mesh: row: 32 (over x, y, z_hi), col: 8 (over z_lo, core).
Axes of the slice: x: 4, y: 4, z: 8 (z_hi: 2, z_lo: 4; z = z_hi * 4 + z_lo), core: 2. Of those that a mesh axis runs over, the one named last changes fastest.
Arguments:
- preacts: bfloat16 [1024, 65536], P('col', 'row'), may hold values from -6 to 6
- resident: bfloat16 [65536, 1024], P('row', 'col'), may hold values from 0 to 0.0101
- ridge: float32 [1], replicated, may hold values from 0.5 to 2
Outputs:
- panel_factor: float32 [2, 256, 65536], P(None, 'col', 'row')
All inputs are finite; a program needn't handle non-finite values.
Results may differ from a plain program's by a relative error of at most 0.0003.
Values may be sent and summed in bfloat16 or wider, within the bound.
A program may use at most 64 MiB of HBM per device.

v0:
```python
import jax
import jax.numpy as jnp
from jax import lax
from jax.sharding import PartitionSpec as P

P_SIZE = 256


def picked(array, axis, root):
    return lax.dynamic_index_in_dim(lax.all_gather(array, axis), root, 0, keepdims=False)


def over_pieces(array, axis):
    return lax.all_gather(array, axis).sum(0)


def in_blocks(array, dim, peers):
    shape = array.shape
    tiles = array.reshape(*shape[:dim], peers, shape[dim] // peers, *shape[dim + 1 :])
    return jnp.moveaxis(tiles, dim, 0)


def sent_and_summed(array, axis, dim):
    peers = lax.axis_size(axis)
    tiles = lax.all_to_all(in_blocks(array, dim, peers), axis, 0, 0, tiled=True)
    return jnp.sum(tiles, axis=0)


def lead_dot(left, right, precision=None):
    return lax.dot_general(
        left,
        right,
        (((0,), (0,)), ((), ())),
        precision=precision,
        preferred_element_type=jnp.float32,
    )


def tail_dot(left, right):
    return lax.dot_general(
        left, right, (((1,), (1,)), ((), ())), preferred_element_type=jnp.float32
    )


def local(preacts, resident, ridge):
    hi = lax.Precision.HIGHEST
    feats = jnp.maximum(preacts, 0)
    ncols = lax.axis_size("col")
    col_index = lax.axis_index("col")
    row_index = lax.axis_index("row")
    rows_dev = feats.shape[1]
    share = P_SIZE // ncols
    samples = feats.shape[0] * ncols
    row_ids = row_index * rows_dev + jnp.arange(rows_dev)
    identity = jnp.eye(P_SIZE, dtype=jnp.float32)
    all_cols, all_rows = (
        picked(feats[:, : 2 * P_SIZE], "row", 0),
        picked(resident[: 2 * P_SIZE, :], "row", 0),
    )
    results = []
    prior_rows = None
    prior_mine = None
    for p in range(2):
        low = p * P_SIZE
        cols = all_cols[:, low : low + P_SIZE]
        frows = all_rows[low : low + P_SIZE]
        diag_term = lead_dot(cols, cols) / samples - tail_dot(frows, frows)
        if p == 1:
            diag_term = diag_term - lead_dot(prior_rows, prior_rows, hi)
        block = over_pieces(diag_term, "col") + ridge[0] * identity
        chol = jnp.linalg.cholesky(block)
        inverse = lax.linalg.triangular_solve(chol, identity, left_side=True, lower=True)

        def strip_term(
            start, count, cols=cols, frows=frows, prior_rows=prior_rows, prior_mine=prior_mine, p=p
        ):
            term = lead_dot(cols, feats) / samples - tail_dot(frows, resident)
            if p == 1:
                term = term - lead_dot(prior_rows, prior_mine, hi)
            return term

        mine_ids = col_index * share + jnp.arange(share)
        whole = strip_term(0, P_SIZE)
        on_diag = (row_ids[None, :] == low + jnp.arange(P_SIZE)[:, None]).astype(jnp.float32)
        whole = whole + jnp.where(col_index == 0, ridge[0], 0.0) * on_diag
        solved = sent_and_summed(
            jnp.dot(inverse, whole, precision=hi, preferred_element_type=jnp.float32), "col", 0
        )
        solved = jnp.where(row_ids[None, :] >= low + mine_ids[:, None], solved, 0.0)
        results.append(solved)
        if p == 0:
            prior_rows = picked(solved[:, P_SIZE : 2 * P_SIZE], "row", 0)
            prior_mine = solved
    return jnp.stack(results)


def solution(mesh):
    placed = (P("col", "row"), P("row", "col"), P())
    return jax.shard_map(
        local, mesh=mesh, in_specs=placed, out_specs=P(None, "col", "row"), check_vma=False
    )
```

profile of v0, /device:TPU:1, one launch (start us, length us, event | category | flops | bytes accessed | tf_op | source)
XLA Modules:
  0.0 668.0 jit_solution(17349682392881862784)
XLA Ops:
  6.5 1.1 broadcast_maximum_fusion
  8.4 1.6 slice.72
  10.1 110.0 %all-gather.11.cloned.1.call-done = bf16[4096,512]{1,0:T(8,128)(2,1)} async-done(((bf16[128,512]{1,0:T(8,128)(2,1)}), bf16[4096,512]{1,0:T(8,128)(2,1)}) %all-gather.11.cloned.1.call-update) | async-done | bytes 4194320 | tf_op jit(solution)/shard_map/all_gather | solution.py:10
  120.0 1.1 convolution_multiply_fusion.3
  121.2 107.7 %all-gather.13.cloned.1.call-done = bf16[16384,128]{1,0:T(8,128)(2,1)} async-done(((bf16[512,128]{1,0:T(8,128)(2,1)}), bf16[16384,128]{1,0:T(8,128)(2,1)}) %all-gather.13.cloned.1.call-update) | async-done | bytes 4194320 | tf_op jit(solution)/shard_map/all_gather | solution.py:10
  228.9 1.8 convolution_subtract_fusion.4
  231.5 1.4 convolution_multiply_fusion.1
  232.9 1.3 fusion.1
  234.2 33.8 %all-gather.15.cloned.1.call-done = f32[2048,256]{1,0:T(8,128)} async-done(((f32[256,256]{1,0:T(8,128)}), f32[2048,256]{1,0:T(8,128)}) %all-gather.15.cloned.1.call-update) | async-done | bytes 2097168 | tf_op jit(solution)/shard_map/all_gather | solution.py:14
  268.0 2.5 reduce_sum.40
  270.5 1.8 copy.6
  272.3 1.7 select_add_fusion.1
  273.9 1.8 copy.7
  277.5 11.7 %cholesky.130 = f32[128,128]{1,0:T(8,128)S(1)} custom-call(f32[128,128]{1,0:T(8,128)S(1)} %cholesky.194), custom_call_target="Cholesky" | custom-call | tf_op jit(solution)/shard_map/jit(cholesky)/cholesky | solution.py:71
  289.3 10.4 %custom-call.13 = f32[1,128,128]{1,2,0:T(8,128)} custom-call(f32[1,128,128]{2,1,0:T(8,128)S(1)} %get-tuple-element.50), custom_call_target="InvertDiagBlocksLowerTriangular" | custom-call | tf_op jit(solution)/shard_map/jit(cholesky)/cholesky | solution.py:71
  300.4 1.7 constant_dynamic-update-slice_fusion.3
  303.2 11.7 %cholesky.147 = f32[128,128]{1,0:T(8,128)S(1)} custom-call(f32[128,128]{1,0:T(8,128)S(1)} %convolution_subtract_fusion.8), custom_call_target="Cholesky" | custom-call | tf_op jit(solution)/shard_map/jit(cholesky)/cholesky | solution.py:71
  317.5 1.7 select_select_fusion.1
  319.9 18.5 %while.4 = (s32[]{:T(128)}, f32[256,256]{1,0:T(8,128)}, s32[2,2]{1,0:T(2,128)S(1)}, f32[2,128,128]{2,1,0:T(8,128)}, s32[]{:T(128)}) while((s32[]{:T(128)}, f32[256,256]{1,0:T(8,128)}, s32[2,2]{1,0:T(2,128)S(1)}, f32[2,128,128]{2,1,0:T(8,128)}, s32[]{:T(128)}) %tuple.44), condition=%wide.while_cond, body=%wide.while_body.sunk | while | flops 2 | bytes 132705 | solution.py:72
  332.3 2.8 bitcast_dynamic-update-slice_fusion.4
  335.7 2.8 bitcast_dynamic-update-slice_fusion.4
  338.4 21.1 %custom-call.14 = f32[2,128,128]{1,2,0:T(8,128)} custom-call(f32[2,128,128]{2,1,0:T(8,128)} %get-tuple-element.21), custom_call_target="InvertDiagBlocksLowerTriangular" | custom-call | tf_op jit(solution)/shard_map/triangular_solve/custom-call.0 | solution.py:72
  359.5 1.1 fusion.16
  360.7 1.2 convolution_subtract_fusion.6
  361.9 1.2 fusion.23
  363.1 3.3 fusion.3
  366.3 5.8 all-to-all-start
  372.2 48.1 %all-to-all-done = f32[8,32,2048]{2,1,0:T(8,128)S(1)} async-done(((f32[8,32,2048]{2,1,0:T(8,128)}), f32[8,32,2048]{2,1,0:T(8,128)S(1)}, u32[]{:S(2)}, u32[]{:S(2)}) %all-to-all-start) | async-done | bytes 2097184 | tf_op jit(solution)/shard_map/all_to_all | solution.py:25
  421.9 1.1 convolution_multiply_fusion.2
  423.0 78.8 %all-gather.17.cloned.1.call-done = f32[1024,256]{1,0:T(8,128)} async-done(((f32[32,256]{1,0:T(8,128)}), f32[1024,256]{1,0:T(8,128)}) %all-gather.17.cloned.1.call-update) | async-done | bytes 1048592 | tf_op jit(solution)/shard_map/all_gather | solution.py:10
  501.8 1.2 fusion.32
  503.0 1.8 fusion.2
  504.9 1.3 convolution_multiply_fusion
  506.2 1.3 convolution_subtract_fusion.1
  507.5 2.8 fusion
  510.3 27.5 %all-gather.19.cloned.1.call-done = f32[2048,256]{1,0:T(8,128)} async-done(((f32[256,256]{1,0:T(8,128)}), f32[2048,256]{1,0:T(8,128)}) %all-gather.19.cloned.1.call-update) | async-done | bytes 2097168 | tf_op jit(solution)/shard_map/all_gather | solution.py:14
  537.8 1.8 reduce_sum.43
  540.0 11.7 %cholesky.164 = f32[128,128]{1,0:T(8,128)S(1)} custom-call(f32[128,128]{1,0:T(8,128)S(1)} %cholesky.197), custom_call_target="Cholesky" | custom-call | tf_op jit(solution)/shard_map/jit(cholesky)/cholesky | solution.py:71
  551.7 9.8 %custom-call.15 = f32[1,128,128]{1,2,0:T(8,128)S(1)} custom-call(f32[1,128,128]{2,1,0:T(8,128)S(1)} %get-tuple-element.46), custom_call_target="InvertDiagBlocksLowerTriangular" | custom-call | tf_op jit(solution)/shard_map/jit(cholesky)/cholesky | solution.py:71
  562.6 1.1 convolution_subtract_fusion.7
  563.7 11.8 %cholesky.181 = f32[128,128]{1,0:T(8,128)S(1)} custom-call(f32[128,128]{1,0:T(8,128)S(1)} %convolution_subtract_fusion.7), custom_call_target="Cholesky" | custom-call | tf_op jit(solution)/shard_map/jit(cholesky)/cholesky | solution.py:71
  578.2 3.9 while.5
  578.8 1.4 bitcast_dynamic-update-slice_fusion.5
  580.8 1.4 bitcast_dynamic-update-slice_fusion.5
  582.2 19.7 %custom-call.16 = f32[2,128,128]{1,2,0:T(8,128)S(1)} custom-call(f32[2,128,128]{2,1,0:T(8,128)S(1)} %get-tuple-element.22), custom_call_target="InvertDiagBlocksLowerTriangular" | custom-call | tf_op jit(solution)/shard_map/triangular_solve/custom-call.0 | solution.py:72
  602.9 3.2 fusion.7
  606.1 5.8 all-to-all-start.1
  612.0 48.1 %all-to-all-done.1 = f32[8,32,2048]{2,1,0:T(8,128)S(1)} async-done(((f32[8,32,2048]{2,1,0:T(8,128)}), f32[8,32,2048]{2,1,0:T(8,128)S(1)}, u32[]{:S(2)}, u32[]{:S(2)}) %all-to-all-start.1) | async-done | bytes 2097184 | tf_op jit(solution)/shard_map/all_to_all | solution.py:25
  (72 shorter events, 15.3 us)
Async XLA Ops:
  6.5 224.9 %copy-start = (bf16[128,2048]{1,0:T(8,128)(2,1)S(1)}, bf16[128,2048]{1,0:T(8,128)(2,1)}, u32[]{:S(2)}) copy-start(bf16[128,2048]{1,0:T(8,128)(2,1)} %param.6) | copy-start | bytes 1572868
  6.5 113.5 %all-gather.11.cloned.1.call-start = ((), (), s32[]{:S(2)}) async-start(), calls=%async_computation.2 | async-start | bytes 4325376 | tf_op jit(solution)/shard_map/all_gather | solution.py:10
  8.4 220.5 %all-gather.13.cloned.1.call-start = ((), (), s32[]{:S(2)}) async-start(), calls=%async_computation.3 | async-start | bytes 4325376 | tf_op jit(solution)/shard_map/all_gather | solution.py:10
  10.0 222.8 %copy-start.1 = (bf16[2048,128]{1,0:T(8,128)(2,1)S(1)}, bf16[2048,128]{1,0:T(8,128)(2,1)}, u32[]{:S(2)}) copy-start(bf16[2048,128]{1,0:T(8,128)(2,1)} %param.7) | copy-start | bytes 1572868
  10.0 258.0 %all-gather.15.cloned.1.call-start = ((), (), s32[]{:S(2)}) async-start(), calls=%async_computation.4 | async-start | bytes 2359296 | tf_op jit(solution)/shard_map/all_gather | solution.py:14
  231.5 129.2 %copy-start.2 = (f32[256,256]{0,1:T(8,128)}, f32[256,256]{0,1:T(8,128)S(1)}, u32[]{:S(2)}) copy-start(f32[256,256]{0,1:T(8,128)S(1)} %fusion.13) | copy-start | bytes 786436
  276.8 0.7 copy-start.7
  366.3 53.9 %all-to-all-start = ((f32[8,32,2048]{2,1,0:T(8,128)}), f32[8,32,2048]{2,1,0:T(8,128)S(1)}, u32[]{:S(2)}, u32[]{:S(2)}) async-start(f32[8,32,2048]{2,1,0:T(8,128)} %bitcast.90), calls=%async_computation | async-start | bytes 4194304 | tf_op jit(solution)/shard_map/all_to_all | solution.py:25
  372.2 129.6 %all-gather.17.cloned.1.call-start = ((), (), s32[]{:S(2)}) async-start(), calls=%async_computation.5 | async-start | bytes 1081344 | tf_op jit(solution)/shard_map/all_gather | solution.py:10
  420.5 0.7 copy-start.4
  421.8 116.0 %all-gather.19.cloned.1.call-start = ((), (), s32[]{:S(2)}) async-start(), calls=%async_computation.6 | async-start | bytes 2359296 | tf_op jit(solution)/shard_map/all_gather | solution.py:14
  506.2 1.3 copy-start.5
  539.7 62.1 %copy-start.3 = (f32[256,256]{0,1:T(8,128)S(1)}, f32[256,256]{0,1:T(8,128)}, u32[]{:S(2)}) copy-start(f32[256,256]{0,1:T(8,128)} %copy-done.2) | copy-start | bytes 786436
  539.9 11.7 %copy-start.6 = (f32[256,256]{1,0:T(8,128)}, f32[256,256]{1,0:T(8,128)S(1)}, u32[]{:S(2)}) copy-start(f32[256,256]{1,0:T(8,128)S(1)} %fusion.11) | copy-start | bytes 786436
  606.1 53.9 %all-to-all-start.1 = ((f32[8,32,2048]{2,1,0:T(8,128)}), f32[8,32,2048]{2,1,0:T(8,128)S(1)}, u32[]{:S(2)}, u32[]{:S(2)}) async-start(f32[8,32,2048]{2,1,0:T(8,128)} %bitcast.91), calls=%async_computation.1 | async-start | bytes 4194304 | tf_op jit(solution)/shard_map/all_to_all | solution.py:25
Sparse Core Ops, SparseCore 0:
  10.8 109.2 all-gather.10
  123.5 105.4 all-gather.12
  230.9 37.0 all-gather.14
  421.9 79.8 all-gather.16
  505.0 32.7 all-gather.18
where the time goes:
time: 672 us; the launch traced here: 668 us
  waiting for transfers between devices  454 us (68%)
  other arithmetic  122 us (18%)
  matrix products  31.2 us (5%)
  local copies, waits for them, and re-layouts  20.2 us (3%)
  between operations  17 us (3%)
  loops' own time  11.9 us (2%)
  starting transfers between devices  11.8 us (2%)
    all_gather x3, waiting for transfers between devices, picked(): lax.all_gather(array, axis)  296 us
    all_to_all x2, waiting for transfers between devices, sent_and_summed(): tiles = lax.all_to_all(in_blocks(array, dim, peers), axis, 0, 0, tiled=True)  96.2 us
    another operation x13, other arithmetic, local(): chol = jnp.linalg.cholesky(block)  69.9 us
    all_gather x2, waiting for transfers between devices, over_pieces(): return lax.all_gather(array, axis).sum(0)  61.3 us
    another operation x5, other arithmetic, local(): lax.linalg.triangular_solve(chol, identity, left_side=True, lower=True)  42.5 us
  transfers between devices with their start and end apart: 7, of which 7 were waited for; matrix products, arithmetic and copies ran while one was open for 2% of the time, Pallas kernels for 0%

commit v1 on v0

v1 whole, which is shorter than its diff:
```python
import jax
import jax.numpy as jnp
from jax import lax
from jax.experimental import pallas as pl
from jax.experimental.pallas import tpu as pltpu
from jax.sharding import PartitionSpec as P

HI = lax.Precision.HIGHEST
F32 = jnp.float32
B16 = jnp.bfloat16

def full(x):
    return jnp.broadcast_to(x, (8, 128))

def base(at, w, sub, lane):
    for k in range(16):
        lo = 8 * k
        tile = at[lo:lo + 8, :]
        cb = [full(tile[:, lo + j:lo + j + 1]) for j in range(8)]
        inblk = (lane >= lo) & (lane < lo + 8)
        rows = jnp.where(inblk, jnp.where(lane - lo == sub, 1.0, 0.0), tile)
        wc = [jnp.where(sub == j, 1.0, 0.0).astype(F32) for j in range(8)]
        piv = []
        diag = jnp.zeros((8, 128), F32)
        for j in range(8):
            d = full(cb[j][j:j + 1, :])
            p = 1.0 / d
            piv.append(p)
            diag = jnp.where(sub == j, d, diag)
            for jj in range(j + 1, 8):
                f = full(cb[j][jj:jj + 1, :]) * p
                cb[jj] = cb[jj] - cb[j] * f
            if j < 7:
                m = jnp.where(sub > j, cb[j] * p, 0.0)
                rows = rows - m * full(rows[j:j + 1, :])
                for jj in range(j + 1):
                    wc[jj] = wc[jj] - m * full(wc[jj][j:j + 1, :])
        w[lo:lo + 8, :] = jnp.where(lane <= lo + sub, rows, 0.0) * lax.rsqrt(diag)
        if k < 15:
            scaled = [full(rows[j:j + 1, :]) * piv[j] for j in range(8)]
            ys = []
            for j in range(8):
                y = scaled[j]
                for jj in range(j + 1, 8):
                    y = y + full(wc[j][jj:jj + 1, :]) * scaled[jj]
                ys.append(y)
            for t in range(k + 1, 16):
                old = at[8 * t:8 * t + 8, :]
                acc = jnp.where(inblk, 0.0, old)
                for j in range(8):
                    acc = acc - full(old[:, lo + j:lo + j + 1]) * ys[j]
                at[8 * t:8 * t + 8, :] = acc

def hdot(a, b, ca=1, cb=0):
    return lax.dot_general(a, b, (((ca,), (cb,)), ((), ())), precision=HI, preferred_element_type=F32)

def bdot(a, b, ca=1, cb=0):
    return lax.dot_general(a, b, (((ca,), (cb,)), ((), ())), preferred_element_type=F32)

def gram(g, lf, lr, aug, ridge):
    for q in range(4):
        cut = slice(128 * q, 128 * (q + 1))
        for c in range(8):
            lr[cut, 128 * c:128 * (c + 1)] = g[c // 2, c % 2, q, 128:256, :]
            f = jnp.maximum(g[c // 2, c % 2, q, 0:128, :], 0)
            lf[cut, 128 * c:128 * (c + 1)] = f.T
    for q in range(4):
        cut = slice(128 * q, 128 * (q + 1))
        a = lf[cut, :]
        r = lr[cut, :]
        s = bdot(a, lf[128 * q:512, :], 1, 1) * (1.0 / 1024) - bdot(r, lr[128 * q:512, :], 1, 1)
        row = lax.broadcasted_iota(jnp.int32, s.shape, 0)
        col = lax.broadcasted_iota(jnp.int32, s.shape, 1)
        aug[cut, 128 * q:512] = s + jnp.where(row == col, ridge, 0.0)

def strip(xf, xr, lf, lr, aug, ridge, first_col):
    f = jnp.maximum(xf[...], 0)
    s = bdot(lf[...], f) * (1.0 / 1024) - bdot(lr[...], xr[...], 1, 1)
    row = lax.broadcasted_iota(jnp.int32, s.shape, 0)
    col = lax.broadcasted_iota(jnp.int32, s.shape, 1) + first_col
    aug[:, 512:768] = s + jnp.where(row == col, ridge, 0.0)

def factor(q, at, w, aug, sub, lane):
    cut = pl.ds(pl.multiple_of(q * 128, 128), 128)
    at[...] = aug[cut, cut]
    base(at, w, sub, lane)

def outer(q, w, aug, out, first_col):
    cut = slice(128 * q, 128 * (q + 1))
    x = hdot(w[...], aug[cut, 128 * (q + 1):768])
    if q < 3:
        aug[cut, 128 * (q + 1):768] = x
        for i in range(q + 1, 4):
            left = aug[cut, 128 * i:128 * (i + 1)]
            rows = slice(128 * i, 128 * (i + 1))
            aug[rows, 128 * i:768] = aug[rows, 128 * i:768] - hdot(left, x[:, 128 * (i - q - 1):], 0, 0)
    mine = x[:, 128 * (3 - q):]
    row = lax.broadcasted_iota(jnp.int32, mine.shape, 0) + 128 * q
    col = lax.broadcasted_iota(jnp.int32, mine.shape, 1) + first_col
    out[...] = jnp.where(col >= row, mine, 0.0)


MESH = pl.DeviceIdType.MESH


def remote(src, dst, send, recv, row, col):
    return pltpu.make_async_remote_copy(
        src_ref=src, dst_ref=dst, send_sem=send, recv_sem=recv, device_id=(row, col), device_id_type=MESH
    )


def kernel(pre, res, rd, out, g, xf, xr, lf, lr, aug, at, w, fin, loc, s1, r1, s2, r2, s3, r3, s4, r4, s5, r5, s6, r6):
    row = lax.axis_index("row")
    col = lax.axis_index("col")
    zhi = lax.rem(row, 2)
    spot = row // 2
    zlo = col // 2
    core = lax.rem(col, 2)
    deep = zhi * 4 + zlo
    other = col + 1 - 2 * core
    ridge = rd[0]
    first_col = row * 2048 + col * 256
    sub = lax.broadcasted_iota(jnp.int32, (8, 128), 0)
    lane = lax.broadcasted_iota(jnp.int32, (8, 128), 1)

    def in_plane(d):
        return 2 * lax.rem(spot + d, 16) + zhi, col

    def in_ring(d):
        z = lax.rem(deep + d, 8)
        return 2 * spot + z // 4, 2 * lax.rem(z, 4) + core

    barrier = pltpu.get_barrier_semaphore()
    peers = [in_plane(d) for d in range(1, 16)] + [in_ring(d) for d in range(1, 8)]
    peers += [(row, 2 * z + 1 - core) for z in range(4)]
    for peer in peers:
        pl.semaphore_signal(barrier, inc=1, device_id=peer, device_id_type=MESH)
    pl.semaphore_wait(barrier, len(peers))

    def piece(q, p):
        if p < 8:
            return pre.at[16 * p:16 * p + 16, 128 * q:128 * q + 128]
        return res.at[128 * q + 16 * (p - 8):128 * q + 16 * (p - 8) + 16, :]

    def scatter(q, p):
        return remote(piece(q, p), g.at[zlo, core, q, 16 * p:16 * p + 16, :], s1.at[q, p], r1.at[q], 2 * p, col)

    def own(q):
        return pltpu.make_async_copy(piece(q, 0), g.at[zlo, core, q, 0:16, :], s1.at[q, 0])

    mine = pl.ds(pl.multiple_of(16 * spot, 16), 16)

    def along_ring(q, d):
        ref = g.at[zlo, core, q, mine, :]
        return remote(ref, ref, s2.at[q, d], r2.at[q, zlo], *in_ring(d))

    def ring_arrival(q, z):
        ref = g.at[z, core, q, mine, :]
        return remote(ref, ref, s2.at[q, 0], r2.at[q, z], row, col)

    def across(q, d):
        ref = g.at[:, core, q, mine, :]
        return remote(ref, ref, s3.at[q, d], r3.at[q, d], *in_plane(d))

    def to_partner(q):
        ref = g.at[:, core, q]
        return remote(ref, ref, s4.at[q], r4.at[q], row, other)

    root = (spot == 0) & (zhi == 0)

    @pl.when(root)
    def _():
        for q in range(4):
            own(q).start()
            for p in range(1, 16):
                scatter(q, p).start()

    for q in range(4):
        @pl.when(zhi == 0)
        def _():
            @pl.when(spot == 0)
            def _():
                own(q).wait()

            @pl.when(spot != 0)
            def _():
                scatter(q, 1).wait_recv()

            for d in range(1, 8):
                along_ring(q, d).start()

    for q in range(4):
        for z in range(4):
            @pl.when((zhi != 0) | (zlo != z))
            def _():
                ring_arrival(q, z).wait_recv()
        for d in range(1, 16):
            across(q, d).start()

    def move_cols(d):
        to = lax.rem(col + d, 8)
        return remote(
            pre.at[:, pl.ds(pl.multiple_of(256 * to, 256), 256)],
            xf.at[pl.ds(pl.multiple_of(128 * col, 128), 128), :], s5.at[0, d], r5.at[0, d], row, to)

    def move_rows(d):
        to = lax.rem(col + d, 8)
        return remote(
            res.at[pl.ds(pl.multiple_of(256 * to, 256), 256), :],
            xr.at[:, pl.ds(pl.multiple_of(128 * col, 128), 128)], s5.at[1, d], r5.at[1, d], row, to)

    keep_cols = pltpu.make_async_copy(
        pre.at[:, pl.ds(pl.multiple_of(256 * col, 256), 256)],
        xf.at[pl.ds(pl.multiple_of(128 * col, 128), 128), :], loc.at[0])
    keep_rows = pltpu.make_async_copy(
        res.at[pl.ds(pl.multiple_of(256 * col, 256), 256), :],
        xr.at[:, pl.ds(pl.multiple_of(128 * col, 128), 128)], loc.at[1])
    keep_cols.start()
    keep_rows.start()
    for d in range(1, 8):
        move_cols(d).start()
        move_rows(d).start()

    for q in range(4):
        for d in range(1, 16):
            across(q, d).wait_recv()
        to_partner(q).start()
    for q in range(4):
        to_partner(q).wait_recv()

    gram(g, lf, lr, aug, ridge)
    keep_cols.wait()
    keep_rows.wait()
    for d in range(1, 8):
        move_cols(d).wait_recv()
        move_rows(d).wait_recv()
    strip(xf, xr, lf, lr, aug, ridge, first_col)

    here = pl.ds(pl.multiple_of(256 * col, 256), 256)

    def deliver(q, i):
        to = 4 * (q % 2) + i
        return remote(
            fin.at[q, 32 * i:32 * i + 32, :], out.at[q // 2, :, here], s6.at[q, i], r6.at[q // 2, col], row, to)

    def keep(q, i):
        return pltpu.make_async_copy(fin.at[q, 32 * i:32 * i + 32, :], out.at[q // 2, :, here], s6.at[q, i])

    def turn(q, carry):
        factor(q, at, w, aug, sub, lane)
        for s in range(4):
            @pl.when(q == s)
            def _():
                outer(s, w, aug, fin.at[s], first_col)
                for i in range(4):
                    to = 4 * (s % 2) + i

                    @pl.when(col == to)
                    def _():
                        keep(s, i).start()

                    @pl.when(col != to)
                    def _():
                        deliver(s, i).start()
        return carry

    lax.fori_loop(0, 4, turn, 0)

    for half in range(2):
        for c in range(8):
            @pl.when(col != c)
            def _():
                ref = out.at[half, :, 256 * c:256 * c + 256]
                remote(fin.at[0, 0:32, :], ref, s6.at[0, 0], r6.at[half, c], row, col).wait_recv()

    for q in range(4):
        for i in range(4):
            to = 4 * (q % 2) + i

            @pl.when(col == to)
            def _():
                keep(q, i).wait()

            @pl.when(col != to)
            def _():
                deliver(q, i).wait_send()
    for d in range(1, 8):
        move_cols(d).wait_send()
        move_rows(d).wait_send()
    for q in range(4):
        to_partner(q).wait_send()
        for d in range(1, 16):
            across(q, d).wait_send()

        @pl.when(zhi == 0)
        def _():
            for d in range(1, 8):
                along_ring(q, d).wait_send()

    @pl.when(root)
    def _():
        for q in range(4):
            for p in range(1, 16):
                scatter(q, p).wait_send()


def local(preacts, resident, ridge):
    dma = pltpu.SemaphoreType.DMA
    return pl.pallas_call(
        kernel,
        out_shape=jax.ShapeDtypeStruct((2, 32, 2048), F32),
        in_specs=[
            pl.BlockSpec(memory_space=pl.ANY),
            pl.BlockSpec(memory_space=pl.ANY),
            pl.BlockSpec(memory_space=pltpu.SMEM),
        ],
        out_specs=pl.BlockSpec(memory_space=pl.ANY),
        scratch_shapes=[
            pltpu.VMEM((4, 2, 4, 256, 128), B16),
            pltpu.VMEM((1024, 256), B16),
            pltpu.VMEM((256, 1024), B16),
            pltpu.VMEM((512, 1024), B16),
            pltpu.VMEM((512, 1024), B16),
            pltpu.VMEM((512, 768), F32),
            pltpu.VMEM((128, 128), F32),
            pltpu.VMEM((128, 128), F32),
            pltpu.VMEM((4, 128, 256), F32),
            dma((2,)),
            dma((4, 16)), dma((4,)),
            dma((4, 8)), dma((4, 4)),
            dma((4, 16)), dma((4, 16)),
            dma((4,)), dma((4,)),
            dma((2, 8)), dma((2, 8)),
            dma((4, 4)), dma((2, 8)),
        ],
        compiler_params=pltpu.CompilerParams(collective_id=0, has_side_effects=True),
    )(preacts, resident, ridge)


def solution(mesh):
    placed = (P("col", "row"), P("row", "col"), P())
    return jax.shard_map(
        local, mesh=mesh, in_specs=placed, out_specs=P(None, "col", "row"), check_vma=False
    )
```

time: 672 us -> 65.8 us (0.10)
  the two profiles are of different devices: /device:TPU:1 before, /device:TPU:85 now
where the time goes in v1:
time: 65.8 us; the launch traced here: 65.6 us
  Pallas kernels  63.1 us (96%)
  local copies, waits for them, and re-layouts  1.87 us (3%)
  between operations  0.66 us (1%)
    pallas_call x1, Pallas kernels, local(): pl.pallas_call(kernel, out_shape=jax.ShapeDtypeStruct((2, 32, 2048), F32)...  63.1 us
    unnamed x1, local copies, waits for them, and re-layouts  1.87 us

profile of v1, /device:TPU:85, one launch (start us, length us, event | category | flops | bytes accessed | tf_op | source)
XLA Modules:
  0.0 65.6 jit_solution(10768905793510829670)
XLA Ops:
  0.7 63.1 %shard_map.37 = f32[2,32,2048]{2,1,0:T(8,128)} custom-call(bf16[128,2048]{1,0:T(8,128)(2,1)} %pre.1, bf16[2048,128]{1,0:T(8,128)(2,1)} %res.1, f32[1]{0:T(128)S(6)} %copy.5.rd), custom_call_target="tpu_custom_call" | custom-call | tf_op jit(solution)/shard_map/pallas_call | solution.py:309
  63.7 1.9 %copy.6 = f32[2,32,2048]{2,1,0:T(8,128)} copy(f32[2,32,2048]{2,1,0:T(8,128)} %shard_map.37) | data formatting | bytes 1048576

commit v2 on v1

v2 whole, which is shorter than its diff:
```python
import jax
import jax.numpy as jnp
from jax import lax
from jax.experimental import pallas as pl
from jax.experimental.pallas import tpu as pltpu
from jax.sharding import PartitionSpec as P

HI = lax.Precision.HIGHEST
F32 = jnp.float32
B16 = jnp.bfloat16

def full(x):
    return jnp.broadcast_to(x, (8, 128))

def row_of(x, j):
    return full(x[j:j + 1, :])


def columns(tile, lo):
    return [full(tile[:, lo + j:lo + j + 1]) for j in range(8)]


def base(at, w, sub, lane, hook=None):
    cb = columns(at[0:8, :], 0)
    for k in range(16):
        lo = 8 * k
        tile = at[lo:lo + 8, :]
        inblk = (lane >= lo) & (lane < lo + 8)
        rows = jnp.where(inblk, jnp.where(lane - lo == sub, 1.0, 0.0), tile)
        wc = [jnp.where(sub == j, 1.0, 0.0).astype(F32) for j in range(8)]
        if k < 15:
            below = at[lo + 8:lo + 16, :]
            first = columns(below, lo)
            nb = columns(below, lo + 8)
            c = list(first)
        piv = []
        diag = jnp.zeros((8, 128), F32)
        for j in range(8):
            d = row_of(cb[j], j)
            p = 1.0 / d
            piv.append(p)
            diag = jnp.where(sub == j, d, diag)
            u = [row_of(cb[j], jj) for jj in range(j + 1, 8)]
            for jj in range(j + 1, 8):
                cb[jj] = cb[jj] - (cb[j] * u[jj - j - 1]) * p
            if k < 15:
                m = c[j] * p
                for jj in range(j + 1, 8):
                    c[jj] = c[jj] - m * u[jj - j - 1]
                for jj in range(8):
                    nb[jj] = nb[jj] - m * row_of(c[j], jj)
            if j < 7:
                m = jnp.where(sub > j, cb[j] * p, 0.0)
                rows = rows - m * row_of(rows, j)
                for jj in range(j + 1):
                    wc[jj] = wc[jj] - m * row_of(wc[jj], j)
        w[lo:lo + 8, :] = jnp.where(lane <= lo + sub, rows, 0.0) * lax.rsqrt(diag)
        if k < 15:
            scaled = [row_of(rows, j) * piv[j] for j in range(8)]
            ys = []
            for j in range(8):
                y = scaled[j]
                for jj in range(j + 1, 8):
                    y = y + row_of(wc[j], jj) * scaled[jj]
                ys.append(y)
            for t in range(k + 1, 16):
                old = at[8 * t:8 * t + 8, :]
                cols = first if t == k + 1 else columns(old, lo)
                parts = [cols[j] * ys[j] for j in range(8)]
                while len(parts) > 1:
                    parts = [a + b for a, b in zip(parts[::2], parts[1::2])]
                at[8 * t:8 * t + 8, :] = jnp.where(inblk, 0.0, old) - parts[0]
            cb = nb
        if hook is not None and k % 4 == 3:
            hook(k // 4)


def hdot(a, b, ca=1, cb=0):
    return lax.dot_general(a, b, (((ca,), (cb,)), ((), ())), precision=HI, preferred_element_type=F32)

def bdot(a, b, ca=1, cb=0):
    return lax.dot_general(a, b, (((ca,), (cb,)), ((), ())), preferred_element_type=F32)

def load_chunk(s, g, lf, lr):
    cut = slice(128 * s, 128 * (s + 1))
    for c in range(8):
        lr[cut, 128 * c:128 * (c + 1)] = g[c // 2, c % 2, s, 128:256, :]
        f = jnp.maximum(g[c // 2, c % 2, s, 0:128, :], 0)
        lf[cut, 128 * c:128 * (c + 1)] = f.T


def diag_block(s, lf, lr, inv, tq, at, ridge):
    cut = slice(128 * s, 128 * (s + 1))
    top = slice(0, 128 * (s + 1))
    d = bdot(lf[top, :], lf[cut, :], 1, 1) * (1.0 / 1024) - bdot(lr[top, :], lr[cut, :], 1, 1)
    own = d[128 * s:, :]
    row = lax.broadcasted_iota(jnp.int32, own.shape, 0)
    col = lax.broadcasted_iota(jnp.int32, own.shape, 1)
    own = own + jnp.where(row == col, ridge, 0.0)
    if s > 0:
        lead = inv[0:128 * s, 0:128 * s]
        x = hdot(lead, d[:128 * s, :])
        own = own - hdot(x, x, 0, 0)
        tq[:, 0:128 * s] = hdot(x, lead, 0, 0)
    at[...] = own


def keep_inverse(s, w, tq, inv):
    cut = slice(128 * s, 128 * (s + 1))
    inv[cut, cut] = w[...]
    if 0 < s < 3:
        inv[cut, 0:128 * s] = -hdot(w[...], tq[:, 0:128 * s])


def strip(s, xf, xr, lf, lr, strips, ridge, first_col):
    cut = slice(128 * s, 128 * (s + 1))
    part = bdot(lf[cut, :], xf[...]) * (1.0 / 1024) - bdot(lr[cut, :], xr[...], 1, 1)
    row = lax.broadcasted_iota(jnp.int32, part.shape, 0) + 128 * s
    col = lax.broadcasted_iota(jnp.int32, part.shape, 1) + first_col
    strips[cut, :] = part + jnp.where(row == col, ridge, 0.0)


MESH = pl.DeviceIdType.MESH


def remote(src, dst, send, recv, row, col):
    return pltpu.make_async_remote_copy(
        src_ref=src, dst_ref=dst, send_sem=send, recv_sem=recv, device_id=(row, col), device_id_type=MESH
    )


def kernel(pre, res, rd, out, g, xf, xr, lf, lr, inv, tq, strips, left, at, w, fin, loc, s1, r1, s2, r2, s3, r3, s4, r4, s5, r5, s6, r6):
    row = lax.axis_index("row")
    col = lax.axis_index("col")
    zhi = lax.rem(row, 2)
    spot = row // 2
    zlo = col // 2
    core = lax.rem(col, 2)
    deep = zhi * 4 + zlo
    other = col + 1 - 2 * core
    ridge = rd[0]
    first_col = row * 2048 + col * 256
    sub = lax.broadcasted_iota(jnp.int32, (8, 128), 0)
    lane = lax.broadcasted_iota(jnp.int32, (8, 128), 1)

    def in_plane(d):
        return 2 * lax.rem(spot + d, 16) + zhi, col

    def in_ring(d):
        z = lax.rem(deep + d, 8)
        return 2 * spot + z // 4, 2 * lax.rem(z, 4) + core

    barrier = pltpu.get_barrier_semaphore()
    peers = [in_plane(d) for d in range(1, 16)] + [in_ring(d) for d in range(1, 8)]
    peers += [(row, 2 * z + 1 - core) for z in range(4)]
    for peer in peers:
        pl.semaphore_signal(barrier, inc=1, device_id=peer, device_id_type=MESH)
    pl.semaphore_wait(barrier, len(peers))

    def piece(q, p):
        if p < 8:
            return pre.at[16 * p:16 * p + 16, 128 * q:128 * q + 128]
        return res.at[128 * q + 16 * (p - 8):128 * q + 16 * (p - 8) + 16, :]

    def scatter(q, p):
        return remote(piece(q, p), g.at[zlo, core, q, 16 * p:16 * p + 16, :], s1.at[q, p], r1.at[q], 2 * p, col)

    def own(q):
        return pltpu.make_async_copy(piece(q, 0), g.at[zlo, core, q, 0:16, :], s1.at[q, 0])

    mine = pl.ds(pl.multiple_of(16 * spot, 16), 16)

    def along_ring(q, d):
        ref = g.at[zlo, core, q, mine, :]
        return remote(ref, ref, s2.at[q, d], r2.at[q, zlo], *in_ring(d))

    def ring_arrival(q, z):
        ref = g.at[z, core, q, mine, :]
        return remote(ref, ref, s2.at[q, 0], r2.at[q, z], row, col)

    def across(q, d):
        ref = g.at[:, core, q, mine, :]
        return remote(ref, ref, s3.at[q, d], r3.at[q, d], *in_plane(d))

    def to_partner(q):
        ref = g.at[:, core, q]
        return remote(ref, ref, s4.at[q], r4.at[q], row, other)

    root = (spot == 0) & (zhi == 0)

    def move_cols(d):
        to = lax.rem(col + d, 8)
        return remote(
            pre.at[:, pl.ds(pl.multiple_of(256 * to, 256), 256)],
            xf.at[pl.ds(pl.multiple_of(128 * col, 128), 128), :], s5.at[0, d], r5.at[0, d], row, to)

    def move_rows(d):
        to = lax.rem(col + d, 8)
        return remote(
            res.at[pl.ds(pl.multiple_of(256 * to, 256), 256), :],
            xr.at[:, pl.ds(pl.multiple_of(128 * col, 128), 128)], s5.at[1, d], r5.at[1, d], row, to)

    keep_cols = pltpu.make_async_copy(
        pre.at[:, pl.ds(pl.multiple_of(256 * col, 256), 256)],
        xf.at[pl.ds(pl.multiple_of(128 * col, 128), 128), :], loc.at[0])
    keep_rows = pltpu.make_async_copy(
        res.at[pl.ds(pl.multiple_of(256 * col, 256), 256), :],
        xr.at[:, pl.ds(pl.multiple_of(128 * col, 128), 128)], loc.at[1])
    here = pl.ds(pl.multiple_of(256 * col, 256), 256)

    def deliver(q, i):
        to = 4 * (q % 2) + i
        return remote(
            fin.at[q, 32 * i:32 * i + 32, :], out.at[q // 2, :, here], s6.at[q, i], r6.at[q // 2, col], row, to)

    def keep(q, i):
        return pltpu.make_async_copy(fin.at[q, 32 * i:32 * i + 32, :], out.at[q // 2, :, here], s6.at[q, i])

    def send_piece(q, i):
        to = 4 * lax.rem(q, 2) + i

        @pl.when(col == to)
        def _():
            keep(q, i).start()

        @pl.when(col != to)
        def _():
            deliver(q, i).start()

    @pl.when(root)
    def _():
        for q in range(4):
            own(q).start()
            for p in range(1, 16):
                scatter(q, p).start()

    keep_cols.start()
    keep_rows.start()
    for d in (1, 2, 6, 7):
        move_cols(d).start()
    inv[...] = jnp.zeros_like(inv)

    def forward_ring(q):
        @pl.when(zhi == 0)
        def _():
            @pl.when(spot == 0)
            def _():
                own(q).wait()

            @pl.when(spot != 0)
            def _():
                scatter(q, 1).wait_recv()

            for d in range(1, 8):
                along_ring(q, d).start()

    def forward_plane(q):
        for z in range(4):
            @pl.when((zhi != 0) | (zlo != z))
            def _():
                ring_arrival(q, z).wait_recv()
        for d in range(1, 16):
            across(q, d).start()

    def share(q):
        for d in range(1, 16):
            across(q, d).wait_recv()
        to_partner(q).start()

    forward_ring(0)
    forward_plane(0)
    for q in range(1, 4):
        forward_ring(q)
    for d in (3, 4, 5):
        move_cols(d).start()
    for d in range(1, 8):
        move_rows(d).start()
    for q in range(1, 4):
        forward_plane(q)
    share(0)

    def arrived():
        keep_cols.wait()
        keep_rows.wait()
        for d in range(1, 8):
            move_cols(d).wait_recv()
            move_rows(d).wait_recv()
        xf[...] = jnp.maximum(xf[...], 0)

    def hook(q, i):
        if i == 1:
            @pl.when(q < 3)
            def _():
                share(q + 1)

        @pl.when(q == 3)
        def _():
            fin[3, 32 * i:32 * i + 32, :] = hdot(w[32 * i:32 * i + 32, :], left[...])
            send_piece(3, i)

    def turn(q, carry):
        for s in range(4):
            @pl.when(q == s)
            def _():
                to_partner(s).wait_recv()
                load_chunk(s, g, lf, lr)
                diag_block(s, lf, lr, inv, tq, at, ridge)
                if s == 3:
                    strip(3, xf, xr, lf, lr, strips, ridge, first_col)
                    left[...] = strips[384:512, :] - hdot(tq[...], strips[0:384, :])
        base(at, w, sub, lane, lambda i: hook(q, i))
        for s in range(3):
            @pl.when(q == s)
            def _():
                keep_inverse(s, w, tq, inv)
                if s == 2:
                    arrived()
                    for e in range(3):
                        strip(e, xf, xr, lf, lr, strips, ridge, first_col)
                        top = 128 * (e + 1)
                        fin[e] = hdot(inv[128 * e:top, 0:top], strips[0:top, :])
                        for i in range(4):
                            send_piece(e, i)
        return carry

    lax.fori_loop(0, 4, turn, 0)

    for half in range(2):
        for c in range(8):
            @pl.when(col != c)
            def _():
                ref = out.at[half, :, 256 * c:256 * c + 256]
                remote(fin.at[0, 0:32, :], ref, s6.at[0, 0], r6.at[half, c], row, col).wait_recv()

    for q in range(4):
        for i in range(4):
            to = 4 * (q % 2) + i

            @pl.when(col == to)
            def _():
                keep(q, i).wait()

            @pl.when(col != to)
            def _():
                deliver(q, i).wait_send()
    for d in range(1, 8):
        move_cols(d).wait_send()
        move_rows(d).wait_send()
    for q in range(4):
        to_partner(q).wait_send()
        for d in range(1, 16):
            across(q, d).wait_send()

        @pl.when(zhi == 0)
        def _():
            for d in range(1, 8):
                along_ring(q, d).wait_send()

    @pl.when(root)
    def _():
        for q in range(4):
            for p in range(1, 16):
                scatter(q, p).wait_send()


def local(preacts, resident, ridge):
    dma = pltpu.SemaphoreType.DMA
    raw = pl.pallas_call(
        kernel,
        out_shape=jax.ShapeDtypeStruct((2, 32, 2048), F32),
        in_specs=[
            pl.BlockSpec(memory_space=pl.ANY),
            pl.BlockSpec(memory_space=pl.ANY),
            pl.BlockSpec(memory_space=pltpu.SMEM),
        ],
        out_specs=pl.BlockSpec(memory_space=pl.ANY),
        scratch_shapes=[
            pltpu.VMEM((4, 2, 4, 256, 128), B16),
            pltpu.VMEM((1024, 256), B16),
            pltpu.VMEM((256, 1024), B16),
            pltpu.VMEM((512, 1024), B16),
            pltpu.VMEM((512, 1024), B16),
            pltpu.VMEM((512, 512), F32),
            pltpu.VMEM((128, 384), F32),
            pltpu.VMEM((512, 256), F32),
            pltpu.VMEM((128, 256), F32),
            pltpu.VMEM((128, 128), F32),
            pltpu.VMEM((128, 128), F32),
            pltpu.VMEM((4, 128, 256), F32),
            dma((2,)),
            dma((4, 16)), dma((4,)),
            dma((4, 8)), dma((4, 4)),
            dma((4, 16)), dma((4, 16)),
            dma((4,)), dma((4,)),
            dma((2, 8)), dma((2, 8)),
            dma((4, 4)), dma((2, 8)),
        ],
        compiler_params=pltpu.CompilerParams(collective_id=0, has_side_effects=True),
    )(preacts, resident, ridge)
    column = lax.axis_index("row") * 2048 + lax.broadcasted_iota(jnp.int32, raw.shape, 2)
    line = lax.broadcasted_iota(jnp.int32, raw.shape, 0) * 256 + lax.broadcasted_iota(jnp.int32, raw.shape, 1)
    return jnp.where(column >= line + lax.axis_index("col") * 32, raw, 0.0)


def solution(mesh):
    placed = (P("col", "row"), P("row", "col"), P())
    return jax.shard_map(
        local, mesh=mesh, in_specs=placed, out_specs=P(None, "col", "row"), check_vma=False
    )
```

time: 65.8 us -> 58.9 us (0.90)
  the two profiles are of different devices: /device:TPU:85 before, /device:TPU:1 now
where the time goes in v2:
time: 58.9 us; the launch traced here: 58.7 us
  Pallas kernels  56.1 us (95%)
  other arithmetic  1.96 us (3%)
  between operations  0.67 us (1%)
    pallas_call x1, Pallas kernels, local(): pl.pallas_call(kernel, out_shape=jax.ShapeDtypeStruct((2, 32, 2048), F32)...  56.1 us
    select_n x1, other arithmetic, local(): return jnp.where(column >= line + lax.axis_index('col') * 32, raw, 0.0)  1.95 us

profile of v2, /device:TPU:1, one launch (start us, length us, event | category | flops | bytes accessed | tf_op | source)
XLA Modules:
  0.0 58.7 jit_solution(17014506416117534023)
XLA Ops:
  0.7 56.1 %shard_map.37 = f32[2,32,2048]{2,1,0:T(8,128)} custom-call(bf16[128,2048]{1,0:T(8,128)(2,1)} %pre.1, bf16[2048,128]{1,0:T(8,128)(2,1)} %res.1, f32[1]{0:T(128)S(6)} %copy.4.rd), custom_call_target="tpu_custom_call" | custom-call | tf_op jit(solution)/shard_map/pallas_call | solution.py:368
  56.8 2.0 %fusion = f32[2,32,2048]{2,1,0:T(8,128)} fusion(f32[2,32,2048]{2,1,0:T(8,128)} %shard_map.37, s32[]{:T(128)S(6)} %mul.16, s32[2]{0:T(128)S(1)} %iota_multiply_fusion, s32[2048]{0:T(1024)S(1)} %iota_add_fusion), kind=kLoop, calls=%fused_computation.1 | loop fusion | flops 524288 | bytes 1056780 | tf_op jit(solution)/shard_map/jit(_where)/select_n | solution.py:402
  (2 shorter events, 0.0 us)

commit v3 on v2

--- a/solution.py
+++ b/solution.py
@@ -89,35 +89,59 @@
         lf[cut, 128 * c:128 * (c + 1)] = f.T
 
 
-def diag_block(s, lf, lr, inv, tq, at, ridge):
-    cut = slice(128 * s, 128 * (s + 1))
-    top = slice(0, 128 * (s + 1))
-    d = bdot(lf[top, :], lf[cut, :], 1, 1) * (1.0 / 1024) - bdot(lr[top, :], lr[cut, :], 1, 1)
-    own = d[128 * s:, :]
-    row = lax.broadcasted_iota(jnp.int32, own.shape, 0)
-    col = lax.broadcasted_iota(jnp.int32, own.shape, 1)
-    own = own + jnp.where(row == col, ridge, 0.0)
-    if s > 0:
-        lead = inv[0:128 * s, 0:128 * s]
-        x = hdot(lead, d[:128 * s, :])
-        own = own - hdot(x, x, 0, 0)
-        tq[:, 0:128 * s] = hdot(x, lead, 0, 0)
-    at[...] = own
-
-
-def keep_inverse(s, w, tq, inv):
-    cut = slice(128 * s, 128 * (s + 1))
-    inv[cut, cut] = w[...]
-    if 0 < s < 3:
-        inv[cut, 0:128 * s] = -hdot(w[...], tq[:, 0:128 * s])
-
-
-def strip(s, xf, xr, lf, lr, strips, ridge, first_col):
-    cut = slice(128 * s, 128 * (s + 1))
-    part = bdot(lf[cut, :], xf[...]) * (1.0 / 1024) - bdot(lr[cut, :], xr[...], 1, 1)
-    row = lax.broadcasted_iota(jnp.int32, part.shape, 0) + 128 * s
-    col = lax.broadcasted_iota(jnp.int32, part.shape, 1) + first_col
-    strips[cut, :] = part + jnp.where(row == col, ridge, 0.0)
+def gram(lf, lr, rows, cols):
+    return bdot(lf[rows, :], lf[cols, :], 1, 1) * (1.0 / 1024) - bdot(lr[rows, :], lr[cols, :], 1, 1)
+
+
+def ridged(x, first_row, first_col, ridge):
+    row = lax.broadcasted_iota(jnp.int32, x.shape, 0) + first_row
+    col = lax.broadcasted_iota(jnp.int32, x.shape, 1) + first_col
+    return x + jnp.where(row == col, ridge, 0.0)
+
+
+def half_block(g, core):
+    total = jnp.zeros((128, 128), F32)
+    rest = jnp.zeros((128, 128), F32)
+    for z in range(4):
+        f = jnp.maximum(g[z, core, 0, 0:128, :], 0)
+        r = g[z, core, 0, 128:256, :]
+        total = total + bdot(f, f, 0, 0)
+        rest = rest + bdot(r, r, 1, 1)
+    return total * (1.0 / 1024) - rest
+
+
+def second_block(w, lf, lr, u01, at, ridge):
+    d = gram(lf, lr, slice(0, 256), slice(128, 256))
+    x = hdot(w[...], d[:128, :])
+    u01[...] = x
+    at[...] = ridged(d[128:, :], 0, 0, ridge) - hdot(x, x, 0, 0)
+
+
+def panels(w0, w, lf, lr, xf, xr, u01, aug, at, fin, ridge, first_col):
+    aug[:, 0:256] = ridged(gram(lf, lr, slice(0, 512), slice(256, 512)), 0, 256, ridge)
+    part = bdot(lf[...], xf[...]) * (1.0 / 1024) - bdot(lr[...], xr[...], 1, 1)
+    aug[:, 256:512] = ridged(part, 0, first_col, ridge)
+    x0 = hdot(w0[...], aug[0:128, :])
+    aug[0:128, :] = x0
+    fin[0] = x0[:, 256:512]
+    x1 = hdot(w[...], aug[128:256, :] - hdot(u01[...], x0, 0, 0))
+    aug[128:256, :] = x1
+    fin[1] = x1[:, 256:512]
+    left = aug[0:256, 0:128]
+    at[...] = aug[256:384, 0:128] - hdot(left, left, 0, 0)
+
+
+def lower_panels(aug):
+    aug[256:384, 128:512] = aug[256:384, 128:512] - hdot(aug[0:256, 0:128], aug[0:256, 128:512], 0, 0)
+    aug[384:512, 128:512] = aug[384:512, 128:512] - hdot(aug[0:256, 128:256], aug[0:256, 128:512], 0, 0)
+
+
+def last_panel(w, aug, at, left, fin):
+    x = hdot(w[...], aug[256:384, 128:512])
+    fin[2] = x[:, 128:384]
+    u = x[:, 0:128]
+    at[...] = aug[384:512, 128:256] - hdot(u, u, 0, 0)
+    left[...] = aug[384:512, 256:512] - hdot(u, x[:, 128:384], 0, 0)
 
 
 MESH = pl.DeviceIdType.MESH
@@ -129,7 +153,7 @@
     )
 
 
-def kernel(pre, res, rd, out, g, xf, xr, lf, lr, inv, tq, strips, left, at, w, fin, loc, s1, r1, s2, r2, s3, r3, s4, r4, s5, r5, s6, r6):
+def kernel(pre, res, rd, out, g, xf, xr, lf, lr, aug, u01, half, left, at, w0, w, fin, loc, s1, r1, s2, r2, s3, r3, s4, r4, s5, r5, s6, r6, s7):
     row = lax.axis_index("row")
     col = lax.axis_index("col")
     zhi = lax.rem(row, 2)
@@ -155,7 +179,8 @@
     peers += [(row, 2 * z + 1 - core) for z in range(4)]
     for peer in peers:
         pl.semaphore_signal(barrier, inc=1, device_id=peer, device_id_type=MESH)
-    pl.semaphore_wait(barrier, len(peers))
+    with jax.named_scope("a_barrier"):
+        pl.semaphore_wait(barrier, len(peers))
 
     def piece(q, p):
         if p < 8:
@@ -238,7 +263,6 @@
     keep_rows.start()
     for d in (1, 2, 6, 7):
         move_cols(d).start()
-    inv[...] = jnp.zeros_like(inv)
 
     def forward_ring(q):
         @pl.when(zhi == 0)
@@ -262,22 +286,33 @@
         for d in range(1, 16):
             across(q, d).start()
 
-    def share(q):
+    def swap():
+        return remote(half.at[0], half.at[1], s7.at[0], s7.at[1], row, other)
+
+    def gathered(q):
         for d in range(1, 16):
             across(q, d).wait_recv()
+
+    def share(q):
+        gathered(q)
         to_partner(q).start()
 
-    forward_ring(0)
-    forward_plane(0)
-    for q in range(1, 4):
-        forward_ring(q)
+    with jax.named_scope("b_ring0"):
+        forward_ring(0)
+    with jax.named_scope("c_plane0"):
+        forward_plane(0)
+    with jax.named_scope("d_ring123"):
+        for q in range(1, 4):
+            forward_ring(q)
     for d in (3, 4, 5):
         move_cols(d).start()
     for d in range(1, 8):
         move_rows(d).start()
-    for q in range(1, 4):
-        forward_plane(q)
-    share(0)
+    with jax.named_scope("e_plane123"):
+        for q in range(1, 4):
+            forward_plane(q)
+    with jax.named_scope("f_gathered0"):
+        gathered(0)
 
     def arrived():
         keep_cols.wait()
@@ -289,9 +324,10 @@
 
     def hook(q, i):
         if i == 1:
-            @pl.when(q < 3)
-            def _():
-                share(q + 1)
+            @pl.when(q < 2)
+            def _():
+                with jax.named_scope("j_share"):
+                    share(q + 1)
 
         @pl.when(q == 3)
         def _():
@@ -299,38 +335,61 @@
             send_piece(3, i)
 
     def turn(q, carry):
-        for s in range(4):
-            @pl.when(q == s)
-            def _():
-                to_partner(s).wait_recv()
-                load_chunk(s, g, lf, lr)
-                diag_block(s, lf, lr, inv, tq, at, ridge)
-                if s == 3:
-                    strip(3, xf, xr, lf, lr, strips, ridge, first_col)
-                    left[...] = strips[384:512, :] - hdot(tq[...], strips[0:384, :])
-        base(at, w, sub, lane, lambda i: hook(q, i))
-        for s in range(3):
-            @pl.when(q == s)
-            def _():
-                keep_inverse(s, w, tq, inv)
-                if s == 2:
-                    arrived()
-                    for e in range(3):
-                        strip(e, xf, xr, lf, lr, strips, ridge, first_col)
-                        top = 128 * (e + 1)
-                        fin[e] = hdot(inv[128 * e:top, 0:top], strips[0:top, :])
-                        for i in range(4):
-                            send_piece(e, i)
+        with jax.named_scope("i_base"):
+            base(at, w, sub, lane, lambda i: hook(q, i))
+
+        @pl.when(q == 0)
+        def _():
+            w0[...] = w[...]
+            with jax.named_scope("k_chunk01"):
+                for s in range(2):
+                    to_partner(s).wait_recv()
+                    load_chunk(s, g, lf, lr)
+            with jax.named_scope("k_second"):
+                second_block(w, lf, lr, u01, at, ridge)
+
+        @pl.when(q == 1)
+        def _():
+            with jax.named_scope("l_chunk23"):
+                share(3)
+                for s in range(2, 4):
+                    to_partner(s).wait_recv()
+                    load_chunk(s, g, lf, lr)
+            with jax.named_scope("l_arrived"):
+                arrived()
+            with jax.named_scope("l_panels"):
+                panels(w0, w, lf, lr, xf, xr, u01, aug, at, fin, ridge, first_col)
+            for e in range(2):
+                for i in range(4):
+                    send_piece(e, i)
+            with jax.named_scope("l_lower"):
+                lower_panels(aug)
+
+        @pl.when(q == 2)
+        def _():
+            with jax.named_scope("m_last"):
+                last_panel(w, aug, at, left, fin)
+            for i in range(4):
+                send_piece(2, i)
+
         return carry
 
+    with jax.named_scope("g_half"):
+        half[0] = half_block(g, core)
+    swap().start()
+    to_partner(0).start()
+    with jax.named_scope("h_swap"):
+        swap().wait_recv()
+    at[...] = ridged(half[0] + half[1], 0, 0, ridge)
     lax.fori_loop(0, 4, turn, 0)
 
-    for half in range(2):
-        for c in range(8):
-            @pl.when(col != c)
-            def _():
-                ref = out.at[half, :, 256 * c:256 * c + 256]
-                remote(fin.at[0, 0:32, :], ref, s6.at[0, 0], r6.at[half, c], row, col).wait_recv()
+    with jax.named_scope("n_final"):
+        for p in range(2):
+            for c in range(8):
+                @pl.when(col != c)
+                def _():
+                    ref = out.at[p, :, 256 * c:256 * c + 256]
+                    remote(fin.at[0, 0:32, :], ref, s6.at[0, 0], r6.at[p, c], row, col).wait_recv()
 
     for q in range(4):
         for i in range(4):
@@ -346,6 +405,7 @@
     for d in range(1, 8):
         move_cols(d).wait_send()
         move_rows(d).wait_send()
+    swap().wait_send()
     for q in range(4):
         to_partner(q).wait_send()
         for d in range(1, 16):
@@ -381,9 +441,10 @@
             pltpu.VMEM((512, 1024), B16),
             pltpu.VMEM((512, 1024), B16),
             pltpu.VMEM((512, 512), F32),
-            pltpu.VMEM((128, 384), F32),
-            pltpu.VMEM((512, 256), F32),
+            pltpu.VMEM((128, 128), F32),
+            pltpu.VMEM((2, 128, 128), F32),
             pltpu.VMEM((128, 256), F32),
+            pltpu.VMEM((128, 128), F32),
             pltpu.VMEM((128, 128), F32),
             pltpu.VMEM((128, 128), F32),
             pltpu.VMEM((4, 128, 256), F32),
@@ -394,6 +455,7 @@
             dma((4,)), dma((4,)),
             dma((2, 8)), dma((2, 8)),
             dma((4, 4)), dma((2, 8)),
+            dma((2,)),
         ],
         compiler_params=pltpu.CompilerParams(collective_id=0, has_side_effects=True),
     )(preacts, resident, ridge)

time: 58.9 us -> 56.9 us (0.966)
  Pallas kernels: 56.1 us -> 54.1 us
    pallas_call x1, Pallas kernels: 56.1 us -> 54.1 us  [local(): pl.pallas_call(kernel, out_shape=jax.ShapeDtypeStruct((2, 32, 2048), F32)...]
where the time goes in v3:
time: 56.9 us; the launch traced here: 56.7 us
  Pallas kernels  54.1 us (95%)
  other arithmetic  1.96 us (3%)
  between operations  0.67 us (1%)
    pallas_call x1, Pallas kernels, local(): pl.pallas_call(kernel, out_shape=jax.ShapeDtypeStruct((2, 32, 2048), F32)...  54.1 us
    select_n x1, other arithmetic, local(): return jnp.where(column >= line + lax.axis_index('col') * 32, raw, 0.0)  1.95 us

profile of v3, /device:TPU:1, one launch (start us, length us, event | category | flops | bytes accessed | tf_op | source)
XLA Modules:
  0.0 56.7 jit_solution(13335063861565591602)
XLA Ops:
  0.7 54.1 %shard_map.37 = f32[2,32,2048]{2,1,0:T(8,128)} custom-call(bf16[128,2048]{1,0:T(8,128)(2,1)} %pre.1, bf16[2048,128]{1,0:T(8,128)(2,1)} %res.1, f32[1]{0:T(128)S(6)} %copy.4.rd), custom_call_target="tpu_custom_call" | custom-call | tf_op jit(solution)/shard_map/pallas_call | solution.py:428
  54.7 2.0 %fusion = f32[2,32,2048]{2,1,0:T(8,128)} fusion(f32[2,32,2048]{2,1,0:T(8,128)} %shard_map.37, s32[]{:T(128)S(6)} %mul.16, s32[2]{0:T(128)S(1)} %iota_multiply_fusion, s32[2048]{0:T(1024)S(1)} %iota_add_fusion), kind=kLoop, calls=%fused_computation.1 | loop fusion | flops 524288 | bytes 1056780 | tf_op jit(solution)/shard_map/jit(_where)/select_n | solution.py:464
  (2 shorter events, 0.0 us)

commit v4 on v3

--- a/solution.py
+++ b/solution.py
@@ -117,16 +117,29 @@
     at[...] = ridged(d[128:, :], 0, 0, ridge) - hdot(x, x, 0, 0)
 
 
-def panels(w0, w, lf, lr, xf, xr, u01, aug, at, fin, ridge, first_col):
-    aug[:, 0:256] = ridged(gram(lf, lr, slice(0, 512), slice(256, 512)), 0, 256, ridge)
-    part = bdot(lf[...], xf[...]) * (1.0 / 1024) - bdot(lr[...], xr[...], 1, 1)
-    aug[:, 256:512] = ridged(part, 0, first_col, ridge)
-    x0 = hdot(w0[...], aug[0:128, :])
-    aug[0:128, :] = x0
-    fin[0] = x0[:, 256:512]
-    x1 = hdot(w[...], aug[128:256, :] - hdot(u01[...], x0, 0, 0))
-    aug[128:256, :] = x1
-    fin[1] = x1[:, 256:512]
+def first_panels(cols, w0, w, u01, aug):
+    x0 = hdot(w0[...], aug[0:128, cols])
+    x1 = hdot(w[...], aug[128:256, cols] - hdot(u01[...], x0, 0, 0))
+    aug[0:128, cols] = x0
+    aug[128:256, cols] = x1
+    return x0, x1
+
+
+def strip(h, w0, w, u01, lf, lr, xf, xr, aug, fin, ridge, first_col):
+    cut = slice(128 * h, 128 * h + 128)
+    cols = slice(256 + 128 * h, 384 + 128 * h)
+    f = jnp.maximum(xf[:, cut], 0)
+    part = bdot(lf[...], f) * (1.0 / 1024) - bdot(lr[...], xr[cut, :], 1, 1)
+    aug[:, cols] = ridged(part, 0, first_col + 128 * h, ridge)
+    x0, x1 = first_panels(cols, w0, w, u01, aug)
+    fin[0, :, cut] = x0
+    fin[1, :, cut] = x1
+
+
+def third_block(w0, w, u01, lf, lr, aug, at, ridge):
+    cols = slice(0, 256)
+    aug[:, cols] = ridged(gram(lf, lr, slice(0, 512), slice(256, 512)), 0, 256, ridge)
+    first_panels(cols, w0, w, u01, aug)
     left = aug[0:256, 0:128]
     at[...] = aug[256:384, 0:128] - hdot(left, left, 0, 0)
 
@@ -153,7 +166,7 @@
     )
 
 
-def kernel(pre, res, rd, out, g, xf, xr, lf, lr, aug, u01, half, left, at, w0, w, fin, loc, s1, r1, s2, r2, s3, r3, s4, r4, s5, r5, s6, r6, s7):
+def kernel(pre, res, rd, out, g, xf, xr, lf, lr, aug, u01, half, left, at, w0, w1, w, fin, s1, r1, s2, r2, s3, r3, s4, r4, s5, r5, s6, r6, s7):
     row = lax.axis_index("row")
     col = lax.axis_index("col")
     zhi = lax.rem(row, 2)
@@ -213,31 +226,43 @@
 
     root = (spot == 0) & (zhi == 0)
 
-    def move_cols(d):
+    def block_of(to, h):
+        return pl.ds(pl.multiple_of(256 * to + 128 * h, 128), 128)
+
+    home = pl.ds(pl.multiple_of(128 * col, 128), 128)
+
+    def places(h):
+        cut = slice(128 * h, 128 * h + 128)
+        return xf.at[home, cut], xr.at[cut, home]
+
+    def move_cols(h, d):
         to = lax.rem(col + d, 8)
-        return remote(
-            pre.at[:, pl.ds(pl.multiple_of(256 * to, 256), 256)],
-            xf.at[pl.ds(pl.multiple_of(128 * col, 128), 128), :], s5.at[0, d], r5.at[0, d], row, to)
-
-    def move_rows(d):
+        return remote(pre.at[:, block_of(to, h)], places(h)[0], s5.at[2 * h, d], r5.at[2 * h, d], row, to)
+
+    def move_rows(h, d):
         to = lax.rem(col + d, 8)
-        return remote(
-            res.at[pl.ds(pl.multiple_of(256 * to, 256), 256), :],
-            xr.at[:, pl.ds(pl.multiple_of(128 * col, 128), 128)], s5.at[1, d], r5.at[1, d], row, to)
-
-    keep_cols = pltpu.make_async_copy(
-        pre.at[:, pl.ds(pl.multiple_of(256 * col, 256), 256)],
-        xf.at[pl.ds(pl.multiple_of(128 * col, 128), 128), :], loc.at[0])
-    keep_rows = pltpu.make_async_copy(
-        res.at[pl.ds(pl.multiple_of(256 * col, 256), 256), :],
-        xr.at[:, pl.ds(pl.multiple_of(128 * col, 128), 128)], loc.at[1])
+        return remote(res.at[block_of(to, h), :], places(h)[1], s5.at[2 * h + 1, d], r5.at[2 * h + 1, d], row, to)
+
+    def stay(h):
+        return [
+            pltpu.make_async_copy(pre.at[:, block_of(col, h)], places(h)[0], s5.at[2 * h, 0]),
+            pltpu.make_async_copy(res.at[block_of(col, h), :], places(h)[1], s5.at[2 * h + 1, 0]),
+        ]
+
     here = pl.ds(pl.multiple_of(256 * col, 256), 256)
 
     def deliver(q, i):
-        to = 4 * (q % 2) + i
+        to = 4 * lax.rem(q, 2) + i
         return remote(
             fin.at[q, 32 * i:32 * i + 32, :], out.at[q // 2, :, here], s6.at[q, i], r6.at[q // 2, col], row, to)
 
+    def deliver_half(q, i, h):
+        to = 4 * lax.rem(q, 2) + i
+        cut = slice(128 * h, 128 * h + 128)
+        lanes = pl.ds(pl.multiple_of(256 * col + 128 * h, 128), 128)
+        return remote(
+            fin.at[q, 32 * i:32 * i + 32, cut], out.at[q // 2, :, lanes], s6.at[q, i], r6.at[q // 2, col], row, to)
+
     def keep(q, i):
         return pltpu.make_async_copy(fin.at[q, 32 * i:32 * i + 32, :], out.at[q // 2, :, here], s6.at[q, i])
 
@@ -251,6 +276,18 @@
         @pl.when(col != to)
         def _():
             deliver(q, i).start()
+
+    def send_half(q, i, h):
+        to = 4 * lax.rem(q, 2) + i
+
+        @pl.when(col != to)
+        def _():
+            deliver_half(q, i, h).start()
+
+        if h == 1:
+            @pl.when(col == to)
+            def _():
+                keep(q, i).start()
 
     @pl.when(root)
     def _():
@@ -259,10 +296,15 @@
             for p in range(1, 16):
                 scatter(q, p).start()
 
-    keep_cols.start()
-    keep_rows.start()
-    for d in (1, 2, 6, 7):
-        move_cols(d).start()
+    for h in range(2):
+        for copy in stay(h):
+            copy.start()
+
+    def move(kind, h, offsets):
+        for d in offsets:
+            kind(h, d).start()
+
+    move(move_cols, 0, (1, 2, 6, 7))
 
     def forward_ring(q):
         @pl.when(zhi == 0)
@@ -299,28 +341,36 @@
 
     with jax.named_scope("b_ring0"):
         forward_ring(0)
+    move(move_cols, 0, (3, 4, 5))
     with jax.named_scope("c_plane0"):
         forward_plane(0)
     with jax.named_scope("d_ring123"):
         for q in range(1, 4):
             forward_ring(q)
-    for d in (3, 4, 5):
-        move_cols(d).start()
-    for d in range(1, 8):
-        move_rows(d).start()
+    move(move_rows, 0, range(1, 8))
+    move(move_cols, 1, range(1, 8))
+    move(move_rows, 1, range(1, 8))
     with jax.named_scope("e_plane123"):
         for q in range(1, 4):
             forward_plane(q)
     with jax.named_scope("f_gathered0"):
         gathered(0)
 
-    def arrived():
-        keep_cols.wait()
-        keep_rows.wait()
+    def arrived(h):
+        for copy in stay(h):
+            copy.wait()
         for d in range(1, 8):
-            move_cols(d).wait_recv()
-            move_rows(d).wait_recv()
-        xf[...] = jnp.maximum(xf[...], 0)
+            move_cols(h, d).wait_recv()
+            move_rows(h, d).wait_recv()
+
+    def solve_half(h):
+        with jax.named_scope("s_arrived"):
+            arrived(h)
+        with jax.named_scope("s_strip"):
+            strip(h, w0, w1, u01, lf, lr, xf, xr, aug, fin, ridge, first_col)
+        for e in range(2):
+            for i in range(4):
+                send_half(e, i, h)
 
     def hook(q, i):
         if i == 1:
@@ -328,6 +378,17 @@
             def _():
                 with jax.named_scope("j_share"):
                     share(q + 1)
+        if i == 2:
+            @pl.when(q == 1)
+            def _():
+                with jax.named_scope("j_share"):
+                    share(3)
+        if i == 0:
+            @pl.when(q == 2)
+            def _():
+                solve_half(1)
+                with jax.named_scope("s_lower"):
+                    lower_panels(aug)
 
         @pl.when(q == 3)
         def _():
@@ -350,20 +411,14 @@
 
         @pl.when(q == 1)
         def _():
+            w1[...] = w[...]
             with jax.named_scope("l_chunk23"):
-                share(3)
                 for s in range(2, 4):
                     to_partner(s).wait_recv()
                     load_chunk(s, g, lf, lr)
-            with jax.named_scope("l_arrived"):
-                arrived()
-            with jax.named_scope("l_panels"):
-                panels(w0, w, lf, lr, xf, xr, u01, aug, at, fin, ridge, first_col)
-            for e in range(2):
-                for i in range(4):
-                    send_piece(e, i)
-            with jax.named_scope("l_lower"):
-                lower_panels(aug)
+            solve_half(0)
+            with jax.named_scope("l_third"):
+                third_block(w0, w1, u01, lf, lr, aug, at, ridge)
 
         @pl.when(q == 2)
         def _():
@@ -402,9 +457,10 @@
             @pl.when(col != to)
             def _():
                 deliver(q, i).wait_send()
-    for d in range(1, 8):
-        move_cols(d).wait_send()
-        move_rows(d).wait_send()
+    for h in range(2):
+        for d in range(1, 8):
+            move_cols(h, d).wait_send()
+            move_rows(h, d).wait_send()
     swap().wait_send()
     for q in range(4):
         to_partner(q).wait_send()
@@ -427,13 +483,13 @@
     dma = pltpu.SemaphoreType.DMA
     raw = pl.pallas_call(
         kernel,
-        out_shape=jax.ShapeDtypeStruct((2, 32, 2048), F32),
+        out_shape=pltpu.VMEM((2, 32, 2048), F32),
         in_specs=[
             pl.BlockSpec(memory_space=pl.ANY),
             pl.BlockSpec(memory_space=pl.ANY),
             pl.BlockSpec(memory_space=pltpu.SMEM),
         ],
-        out_specs=pl.BlockSpec(memory_space=pl.ANY),
+        out_specs=pl.BlockSpec(memory_space=pltpu.VMEM),
         scratch_shapes=[
             pltpu.VMEM((4, 2, 4, 256, 128), B16),
             pltpu.VMEM((1024, 256), B16),
@@ -447,13 +503,13 @@
             pltpu.VMEM((128, 128), F32),
             pltpu.VMEM((128, 128), F32),
             pltpu.VMEM((128, 128), F32),
+            pltpu.VMEM((128, 128), F32),
             pltpu.VMEM((4, 128, 256), F32),
-            dma((2,)),
             dma((4, 16)), dma((4,)),
             dma((4, 8)), dma((4, 4)),
             dma((4, 16)), dma((4, 16)),
             dma((4,)), dma((4,)),
-            dma((2, 8)), dma((2, 8)),
+            dma((4, 8)), dma((4, 8)),
             dma((4, 4)), dma((2, 8)),
             dma((2,)),
         ],

time: 56.9 us -> 56.4 us (level)
  other arithmetic: 1.96 us -> 0.92 us
  Pallas kernels: 54.1 us -> 54.7 us
    select_n x1, other arithmetic: 1.95 us -> 0.91 us  [local(): return jnp.where(column >= line + lax.axis_index('col') * 32, raw, 0.0)]
    pallas_call x1, Pallas kernels: 54.1 us -> 54.7 us  [local(): pl.pallas_call(kernel, out_shape=pltpu.VMEM((2, 32, 2048), F32), in_specs...]
where the time goes in v4:
time: 56.4 us; the launch traced here: 56.2 us
  Pallas kernels  54.7 us (97%)
  other arithmetic  0.92 us (2%)
  between operations  0.67 us (1%)
    pallas_call x1, Pallas kernels, local(): pl.pallas_call(kernel, out_shape=pltpu.VMEM((2, 32, 2048), F32), in_specs...  54.7 us

profile of v4, /device:TPU:1, one launch (start us, length us, event | category | flops | bytes accessed | tf_op | source)
XLA Modules:
  0.0 56.2 jit_solution(17904732893802496868)
XLA Ops:
  0.7 54.7 %shard_map.37 = f32[2,32,2048]{2,1,0:T(8,128)S(1)} custom-call(bf16[128,2048]{1,0:T(8,128)(2,1)} %pre.1, bf16[2048,128]{1,0:T(8,128)(2,1)} %res.1, f32[1]{0:T(128)S(6)} %copy.4.rd), custom_call_target="tpu_custom_call" | custom-call | tf_op jit(solution)/shard_map/pallas_call | solution.py:484
  55.3 0.9 %fusion = f32[2,32,2048]{2,1,0:T(8,128)} fusion(f32[2,32,2048]{2,1,0:T(8,128)S(1)} %shard_map.37, s32[]{:T(128)S(6)} %mul.16, s32[2]{0:T(128)S(1)} %iota_multiply_fusion, s32[2048]{0:T(1024)S(1)} %iota_add_fusion), kind=kLoop, calls=%fused_computation.1 | loop fusion | flops 524288 | bytes 1056780 | tf_op jit(solution)/shard_map/jit(_where)/select_n | solution.py:520
  (2 shorter events, 0.0 us)

commit v5 on v4

--- a/solution.py
+++ b/solution.py
@@ -125,15 +125,13 @@
     return x0, x1
 
 
-def strip(h, w0, w, u01, lf, lr, xf, xr, aug, fin, ridge, first_col):
-    cut = slice(128 * h, 128 * h + 128)
-    cols = slice(256 + 128 * h, 384 + 128 * h)
-    f = jnp.maximum(xf[:, cut], 0)
-    part = bdot(lf[...], f) * (1.0 / 1024) - bdot(lr[...], xr[cut, :], 1, 1)
-    aug[:, cols] = ridged(part, 0, first_col + 128 * h, ridge)
+def strip(w0, w, u01, lf, lr, xf, xr, aug, fin, ridge, first_col):
+    cols = slice(256, 512)
+    part = bdot(lf[...], jnp.maximum(xf[...], 0)) * (1.0 / 1024) - bdot(lr[...], xr[...], 1, 1)
+    aug[:, cols] = ridged(part, 0, first_col, ridge)
     x0, x1 = first_panels(cols, w0, w, u01, aug)
-    fin[0, :, cut] = x0
-    fin[1, :, cut] = x1
+    fin[0] = x0
+    fin[1] = x1
 
 
 def third_block(w0, w, u01, lf, lr, aug, at, ridge):
@@ -166,7 +164,7 @@
     )
 
 
-def kernel(pre, res, rd, out, g, xf, xr, lf, lr, aug, u01, half, left, at, w0, w1, w, fin, s1, r1, s2, r2, s3, r3, s4, r4, s5, r5, s6, r6, s7):
+def kernel(pre, res, rd, out, g, xf, xr, lf, lr, aug, u01, half, left, at, w0, w1, w, fin, loc, sent, r1, r2, r3, r4, r5, r6, s7):
     row = lax.axis_index("row")
     col = lax.axis_index("col")
     zhi = lax.rem(row, 2)
@@ -201,70 +199,54 @@
         return res.at[128 * q + 16 * (p - 8):128 * q + 16 * (p - 8) + 16, :]
 
     def scatter(q, p):
-        return remote(piece(q, p), g.at[zlo, core, q, 16 * p:16 * p + 16, :], s1.at[q, p], r1.at[q], 2 * p, col)
+        return remote(piece(q, p), g.at[zlo, core, q, 16 * p:16 * p + 16, :], sent.at[0], r1.at[q], 2 * p, col)
 
     def own(q):
-        return pltpu.make_async_copy(piece(q, 0), g.at[zlo, core, q, 0:16, :], s1.at[q, 0])
+        return pltpu.make_async_copy(piece(q, 0), g.at[zlo, core, q, 0:16, :], r1.at[q])
 
     mine = pl.ds(pl.multiple_of(16 * spot, 16), 16)
 
     def along_ring(q, d):
         ref = g.at[zlo, core, q, mine, :]
-        return remote(ref, ref, s2.at[q, d], r2.at[q, zlo], *in_ring(d))
-
-    def ring_arrival(q, z):
-        ref = g.at[z, core, q, mine, :]
-        return remote(ref, ref, s2.at[q, 0], r2.at[q, z], row, col)
+        return remote(ref, ref, sent.at[1], r2.at[q], *in_ring(d))
 
     def across(q, d):
         ref = g.at[:, core, q, mine, :]
-        return remote(ref, ref, s3.at[q, d], r3.at[q, d], *in_plane(d))
+        return remote(ref, ref, sent.at[2], r3.at[q], *in_plane(d))
 
     def to_partner(q):
         ref = g.at[:, core, q]
-        return remote(ref, ref, s4.at[q], r4.at[q], row, other)
+        return remote(ref, ref, sent.at[3], r4.at[q], row, other)
+
+    def bulk(ref, sem):
+        return remote(ref, ref, sem, sem, row, other)
 
     root = (spot == 0) & (zhi == 0)
 
-    def block_of(to, h):
-        return pl.ds(pl.multiple_of(256 * to + 128 * h, 128), 128)
+    def block_of(to):
+        return pl.ds(pl.multiple_of(256 * to, 256), 256)
 
     home = pl.ds(pl.multiple_of(128 * col, 128), 128)
 
-    def places(h):
-        cut = slice(128 * h, 128 * h + 128)
-        return xf.at[home, cut], xr.at[cut, home]
-
-    def move_cols(h, d):
+    def move_cols(d):
         to = lax.rem(col + d, 8)
-        return remote(pre.at[:, block_of(to, h)], places(h)[0], s5.at[2 * h, d], r5.at[2 * h, d], row, to)
-
-    def move_rows(h, d):
+        return remote(pre.at[:, block_of(to)], xf.at[home, :], sent.at[4], r5.at[0], row, to)
+
+    def move_rows(d):
         to = lax.rem(col + d, 8)
-        return remote(res.at[block_of(to, h), :], places(h)[1], s5.at[2 * h + 1, d], r5.at[2 * h + 1, d], row, to)
-
-    def stay(h):
-        return [
-            pltpu.make_async_copy(pre.at[:, block_of(col, h)], places(h)[0], s5.at[2 * h, 0]),
-            pltpu.make_async_copy(res.at[block_of(col, h), :], places(h)[1], s5.at[2 * h + 1, 0]),
-        ]
+        return remote(res.at[block_of(to), :], xr.at[:, home], sent.at[5], r5.at[1], row, to)
+
+    keep_cols = pltpu.make_async_copy(pre.at[:, block_of(col)], xf.at[home, :], loc.at[0])
+    keep_rows = pltpu.make_async_copy(res.at[block_of(col), :], xr.at[:, home], loc.at[1])
 
     here = pl.ds(pl.multiple_of(256 * col, 256), 256)
 
     def deliver(q, i):
         to = 4 * lax.rem(q, 2) + i
-        return remote(
-            fin.at[q, 32 * i:32 * i + 32, :], out.at[q // 2, :, here], s6.at[q, i], r6.at[q // 2, col], row, to)
-
-    def deliver_half(q, i, h):
-        to = 4 * lax.rem(q, 2) + i
-        cut = slice(128 * h, 128 * h + 128)
-        lanes = pl.ds(pl.multiple_of(256 * col + 128 * h, 128), 128)
-        return remote(
-            fin.at[q, 32 * i:32 * i + 32, cut], out.at[q // 2, :, lanes], s6.at[q, i], r6.at[q // 2, col], row, to)
+        return remote(fin.at[q, 32 * i:32 * i + 32, :], out.at[q // 2, :, here], sent.at[6], r6.at[0], row, to)
 
     def keep(q, i):
-        return pltpu.make_async_copy(fin.at[q, 32 * i:32 * i + 32, :], out.at[q // 2, :, here], s6.at[q, i])
+        return pltpu.make_async_copy(fin.at[q, 32 * i:32 * i + 32, :], out.at[q // 2, :, here], loc.at[2])
 
     def send_piece(q, i):
         to = 4 * lax.rem(q, 2) + i
@@ -276,18 +258,6 @@
         @pl.when(col != to)
         def _():
             deliver(q, i).start()
-
-    def send_half(q, i, h):
-        to = 4 * lax.rem(q, 2) + i
-
-        @pl.when(col != to)
-        def _():
-            deliver_half(q, i, h).start()
-
-        if h == 1:
-            @pl.when(col == to)
-            def _():
-                keep(q, i).start()
 
     @pl.when(root)
     def _():
@@ -296,15 +266,14 @@
             for p in range(1, 16):
                 scatter(q, p).start()
 
-    for h in range(2):
-        for copy in stay(h):
-            copy.start()
-
-    def move(kind, h, offsets):
+    keep_cols.start()
+    keep_rows.start()
+
+    def move(kind, offsets):
         for d in offsets:
-            kind(h, d).start()
-
-    move(move_cols, 0, (1, 2, 6, 7))
+            kind(d).start()
+
+    move(move_cols, (1, 7))
 
     def forward_ring(q):
         @pl.when(zhi == 0)
@@ -321,10 +290,14 @@
                 along_ring(q, d).start()
 
     def forward_plane(q):
-        for z in range(4):
-            @pl.when((zhi != 0) | (zlo != z))
-            def _():
-                ring_arrival(q, z).wait_recv()
+        @pl.when(zhi == 0)
+        def _():
+            bulk(g.at[0:3, core, q, mine, :], r2.at[q]).wait_recv()
+
+        @pl.when(zhi != 0)
+        def _():
+            bulk(g.at[:, core, q, mine, :], r2.at[q]).wait_recv()
+
         for d in range(1, 16):
             across(q, d).start()
 
@@ -332,8 +305,7 @@
         return remote(half.at[0], half.at[1], s7.at[0], s7.at[1], row, other)
 
     def gathered(q):
-        for d in range(1, 16):
-            across(q, d).wait_recv()
+        bulk(g.at[:, core, q, 0:240, :], r3.at[q]).wait_recv()
 
     def share(q):
         gathered(q)
@@ -341,36 +313,24 @@
 
     with jax.named_scope("b_ring0"):
         forward_ring(0)
-    move(move_cols, 0, (3, 4, 5))
+    move(move_cols, (2, 6))
     with jax.named_scope("c_plane0"):
         forward_plane(0)
     with jax.named_scope("d_ring123"):
         for q in range(1, 4):
             forward_ring(q)
-    move(move_rows, 0, range(1, 8))
-    move(move_cols, 1, range(1, 8))
-    move(move_rows, 1, range(1, 8))
-    with jax.named_scope("e_plane123"):
-        for q in range(1, 4):
-            forward_plane(q)
+    move(move_cols, (3, 4, 5))
+    move(move_rows, range(1, 8))
+    with jax.named_scope("e_plane1"):
+        forward_plane(1)
     with jax.named_scope("f_gathered0"):
         gathered(0)
 
-    def arrived(h):
-        for copy in stay(h):
-            copy.wait()
-        for d in range(1, 8):
-            move_cols(h, d).wait_recv()
-            move_rows(h, d).wait_recv()
-
-    def solve_half(h):
-        with jax.named_scope("s_arrived"):
-            arrived(h)
-        with jax.named_scope("s_strip"):
-            strip(h, w0, w1, u01, lf, lr, xf, xr, aug, fin, ridge, first_col)
-        for e in range(2):
-            for i in range(4):
-                send_half(e, i, h)
+    def arrived():
+        keep_cols.wait()
+        keep_rows.wait()
+        bulk(xf.at[0:896, :], r5.at[0]).wait_recv()
+        bulk(xr.at[:, 0:896], r5.at[1]).wait_recv()
 
     def hook(q, i):
         if i == 1:
@@ -386,7 +346,13 @@
         if i == 0:
             @pl.when(q == 2)
             def _():
-                solve_half(1)
+                with jax.named_scope("s_arrived"):
+                    arrived()
+                with jax.named_scope("s_strip"):
+                    strip(w0, w1, u01, lf, lr, xf, xr, aug, fin, ridge, first_col)
+                for e in range(2):
+                    for n in range(4):
+                        send_piece(e, n)
                 with jax.named_scope("s_lower"):
                     lower_panels(aug)
 
@@ -416,7 +382,6 @@
                 for s in range(2, 4):
                     to_partner(s).wait_recv()
                     load_chunk(s, g, lf, lr)
-            solve_half(0)
             with jax.named_scope("l_third"):
                 third_block(w0, w1, u01, lf, lr, aug, at, ridge)
 
@@ -433,50 +398,32 @@
         half[0] = half_block(g, core)
     swap().start()
     to_partner(0).start()
+    with jax.named_scope("g_plane23"):
+        forward_plane(2)
+        forward_plane(3)
     with jax.named_scope("h_swap"):
         swap().wait_recv()
     at[...] = ridged(half[0] + half[1], 0, 0, ridge)
     lax.fori_loop(0, 4, turn, 0)
 
     with jax.named_scope("n_final"):
-        for p in range(2):
-            for c in range(8):
-                @pl.when(col != c)
-                def _():
-                    ref = out.at[p, :, 256 * c:256 * c + 256]
-                    remote(fin.at[0, 0:32, :], ref, s6.at[0, 0], r6.at[p, c], row, col).wait_recv()
-
-    for q in range(4):
-        for i in range(4):
-            to = 4 * (q % 2) + i
-
-            @pl.when(col == to)
-            def _():
-                keep(q, i).wait()
-
-            @pl.when(col != to)
-            def _():
-                deliver(q, i).wait_send()
-    for h in range(2):
-        for d in range(1, 8):
-            move_cols(h, d).wait_send()
-            move_rows(h, d).wait_send()
-    swap().wait_send()
-    for q in range(4):
-        to_partner(q).wait_send()
-        for d in range(1, 16):
-            across(q, d).wait_send()
+        bulk(fin.at[:, 0:112, :], r6.at[0]).wait_recv()
+    with jax.named_scope("o_sends"):
+        pltpu.make_async_copy(fin.at[0, 0:64, :], fin.at[1, 0:64, :], loc.at[2]).wait()
+        bulk(fin.at[:, 0:112, :], sent.at[6]).wait_send()
+        bulk(xf.at[0:896, :], sent.at[4]).wait_send()
+        bulk(xr.at[:, 0:896], sent.at[5]).wait_send()
+        swap().wait_send()
+        bulk(g.at[:, core], sent.at[3]).wait_send()
+        bulk(g.at[:, core, :, 0:240, :], sent.at[2]).wait_send()
 
         @pl.when(zhi == 0)
         def _():
-            for d in range(1, 8):
-                along_ring(q, d).wait_send()
-
-    @pl.when(root)
-    def _():
-        for q in range(4):
-            for p in range(1, 16):
-                scatter(q, p).wait_send()
+            bulk(g.at[0, core, :, 0:112, :], sent.at[1]).wait_send()
+
+        @pl.when(root)
+        def _():
+            bulk(g.at[:, core, 0, 0:240, :], sent.at[0]).wait_send()
 
 
 def local(preacts, resident, ridge):
@@ -505,13 +452,9 @@
             pltpu.VMEM((128, 128), F32),
             pltpu.VMEM((128, 128), F32),
             pltpu.VMEM((4, 128, 256), F32),
-            dma((4, 16)), dma((4,)),
-            dma((4, 8)), dma((4, 4)),
-            dma((4, 16)), dma((4, 16)),
-            dma((4,)), dma((4,)),
-            dma((4, 8)), dma((4, 8)),
-            dma((4, 4)), dma((2, 8)),
-            dma((2,)),
+            dma((3,)), dma((7,)),
+            dma((4,)), dma((4,)), dma((4,)), dma((4,)),
+            dma((2,)), dma((1,)), dma((2,)),
         ],
         compiler_params=pltpu.CompilerParams(collective_id=0, has_side_effects=True),
     )(preacts, resident, ridge)

time: 56.4 us -> 53.4 us (0.947)
  Pallas kernels: 54.7 us -> 51.7 us
    pallas_call x1, Pallas kernels: 54.7 us -> 51.7 us  [local(): pl.pallas_call(kernel, out_shape=pltpu.VMEM((2, 32, 2048), F32), in_specs...]
where the time goes in v5:
time: 53.4 us; the launch traced here: 53.3 us
  Pallas kernels  51.7 us (97%)
  other arithmetic  0.92 us (2%)
  between operations  0.67 us (1%)
    pallas_call x1, Pallas kernels, local(): pl.pallas_call(kernel, out_shape=pltpu.VMEM((2, 32, 2048), F32), in_specs...  51.7 us

profile of v5, /device:TPU:1, one launch (start us, length us, event | category | flops | bytes accessed | tf_op | source)
XLA Modules:
  0.0 53.3 jit_solution(1138621022803599947)
XLA Ops:
  0.7 51.7 %shard_map.37 = f32[2,32,2048]{2,1,0:T(8,128)S(1)} custom-call(bf16[128,2048]{1,0:T(8,128)(2,1)} %pre.1, bf16[2048,128]{1,0:T(8,128)(2,1)} %res.1, f32[1]{0:T(128)S(6)} %copy.4.rd), custom_call_target="tpu_custom_call" | custom-call | tf_op jit(solution)/shard_map/pallas_call | solution.py:431
  52.4 0.9 %fusion = f32[2,32,2048]{2,1,0:T(8,128)} fusion(f32[2,32,2048]{2,1,0:T(8,128)S(1)} %shard_map.37, s32[]{:T(128)S(6)} %mul.16, s32[2]{0:T(128)S(1)} %iota_multiply_fusion, s32[2048]{0:T(1024)S(1)} %iota_add_fusion), kind=kLoop, calls=%fused_computation.1 | loop fusion | flops 524288 | bytes 1056780 | tf_op jit(solution)/shard_map/jit(_where)/select_n | solution.py:463
  (2 shorter events, 0.0 us)

commit v6 on v5

--- a/solution.py
+++ b/solution.py
@@ -20,7 +20,7 @@
     return [full(tile[:, lo + j:lo + j + 1]) for j in range(8)]
 
 
-def base(at, w, sub, lane, hook=None):
+def base(at, w, sub, lane, hook):
     cb = columns(at[0:8, :], 0)
     for k in range(16):
         lo = 8 * k
@@ -71,12 +71,26 @@
                     parts = [a + b for a, b in zip(parts[::2], parts[1::2])]
                 at[8 * t:8 * t + 8, :] = jnp.where(inblk, 0.0, old) - parts[0]
             cb = nb
-        if hook is not None and k % 4 == 3:
+        if k % 4 == 3:
             hook(k // 4)
 
 
 def hdot(a, b, ca=1, cb=0):
-    return lax.dot_general(a, b, (((ca,), (cb,)), ((), ())), precision=HI, preferred_element_type=F32)
+    if b.shape[1 - cb] < 256:
+        return lax.dot_general(a, b, (((ca,), (cb,)), ((), ())), precision=HI, preferred_element_type=F32)
+    a0, a1, a2 = thirds(a)
+    b0, b1, b2 = thirds(b)
+    left = jnp.concatenate([a0, a0, a0, a1, a1, a2], axis=ca)
+    right = jnp.concatenate([b0, b1, b2, b0, b1, b0], axis=cb)
+    return bdot(left, right, ca, cb)
+
+
+def thirds(x):
+    x0 = x.astype(B16)
+    rest = x - x0.astype(F32)
+    x1 = rest.astype(B16)
+    return x0, x1, (rest - x1.astype(F32)).astype(B16)
+
 
 def bdot(a, b, ca=1, cb=0):
     return lax.dot_general(a, b, (((ca,), (cb,)), ((), ())), preferred_element_type=F32)
@@ -125,24 +139,31 @@
     return x0, x1
 
 
-def strip(w0, w, u01, lf, lr, xf, xr, aug, fin, ridge, first_col):
-    cols = slice(256, 512)
-    part = bdot(lf[...], jnp.maximum(xf[...], 0)) * (1.0 / 1024) - bdot(lr[...], xr[...], 1, 1)
-    aug[:, cols] = ridged(part, 0, first_col, ridge)
-    x0, x1 = first_panels(cols, w0, w, u01, aug)
+def strip(rows, lf, lr, xf, xr, aug, ridge, first_col):
+    part = bdot(lf[rows, :], jnp.maximum(xf[...], 0)) * (1.0 / 1024) - bdot(lr[rows, :], xr[...], 1, 1)
+    aug[rows, 256:512] = ridged(part, rows.start, first_col, ridge)
+
+
+def upper_strip(w0, w, u01, lf, lr, xf, xr, aug, fin, ridge, first_col):
+    strip(slice(0, 256), lf, lr, xf, xr, aug, ridge, first_col)
+    x0, x1 = first_panels(slice(256, 512), w0, w, u01, aug)
     fin[0] = x0
     fin[1] = x1
 
 
 def third_block(w0, w, u01, lf, lr, aug, at, ridge):
-    cols = slice(0, 256)
-    aug[:, cols] = ridged(gram(lf, lr, slice(0, 512), slice(256, 512)), 0, 256, ridge)
+    cols = slice(0, 128)
+    aug[0:384, cols] = ridged(gram(lf, lr, slice(0, 384), slice(256, 384)), 0, 256, ridge)
     first_panels(cols, w0, w, u01, aug)
-    left = aug[0:256, 0:128]
-    at[...] = aug[256:384, 0:128] - hdot(left, left, 0, 0)
-
-
-def lower_panels(aug):
+    left = aug[0:256, cols]
+    at[...] = aug[256:384, cols] - hdot(left, left, 0, 0)
+
+
+def lower_panels(w0, w, u01, lf, lr, xf, xr, aug, ridge, first_col):
+    cols = slice(128, 256)
+    aug[:, cols] = ridged(gram(lf, lr, slice(0, 512), slice(384, 512)), 0, 384, ridge)
+    first_panels(cols, w0, w, u01, aug)
+    strip(slice(256, 512), lf, lr, xf, xr, aug, ridge, first_col)
     aug[256:384, 128:512] = aug[256:384, 128:512] - hdot(aug[0:256, 0:128], aug[0:256, 128:512], 0, 0)
     aug[384:512, 128:512] = aug[384:512, 128:512] - hdot(aug[0:256, 128:256], aug[0:256, 128:512], 0, 0)
 
@@ -242,14 +263,14 @@
     here = pl.ds(pl.multiple_of(256 * col, 256), 256)
 
     def deliver(q, i):
-        to = 4 * lax.rem(q, 2) + i
+        to = 4 * (q % 2) + i
         return remote(fin.at[q, 32 * i:32 * i + 32, :], out.at[q // 2, :, here], sent.at[6], r6.at[0], row, to)
 
     def keep(q, i):
         return pltpu.make_async_copy(fin.at[q, 32 * i:32 * i + 32, :], out.at[q // 2, :, here], loc.at[2])
 
     def send_piece(q, i):
-        to = 4 * lax.rem(q, 2) + i
+        to = 4 * (q % 2) + i
 
         @pl.when(col == to)
         def _():
@@ -273,7 +294,14 @@
         for d in offsets:
             kind(d).start()
 
-    move(move_cols, (1, 7))
+    @pl.when(zhi != 0)
+    def _():
+        move(move_cols, range(1, 8))
+        move(move_rows, range(1, 8))
+
+    @pl.when(zhi == 0)
+    def _():
+        move(move_cols, (1, 7))
 
     def forward_ring(q):
         @pl.when(zhi == 0)
@@ -313,14 +341,22 @@
 
     with jax.named_scope("b_ring0"):
         forward_ring(0)
-    move(move_cols, (2, 6))
+
+    @pl.when(zhi == 0)
+    def _():
+        move(move_cols, (2, 6, 4))
+
     with jax.named_scope("c_plane0"):
         forward_plane(0)
     with jax.named_scope("d_ring123"):
         for q in range(1, 4):
             forward_ring(q)
-    move(move_cols, (3, 4, 5))
-    move(move_rows, range(1, 8))
+
+    @pl.when(zhi == 0)
+    def _():
+        move(move_cols, (3, 5))
+        move(move_rows, range(1, 8))
+
     with jax.named_scope("e_plane1"):
         forward_plane(1)
     with jax.named_scope("f_gathered0"):
@@ -332,38 +368,19 @@
         bulk(xf.at[0:896, :], r5.at[0]).wait_recv()
         bulk(xr.at[:, 0:896], r5.at[1]).wait_recv()
 
-    def hook(q, i):
+    def early_hook(q, i):
         if i == 1:
-            @pl.when(q < 2)
-            def _():
-                with jax.named_scope("j_share"):
-                    share(q + 1)
+            with jax.named_scope("j_share"):
+                share(q + 1)
         if i == 2:
             @pl.when(q == 1)
             def _():
-                with jax.named_scope("j_share"):
+                with jax.named_scope("j_share3"):
                     share(3)
-        if i == 0:
-            @pl.when(q == 2)
-            def _():
-                with jax.named_scope("s_arrived"):
-                    arrived()
-                with jax.named_scope("s_strip"):
-                    strip(w0, w1, u01, lf, lr, xf, xr, aug, fin, ridge, first_col)
-                for e in range(2):
-                    for n in range(4):
-                        send_piece(e, n)
-                with jax.named_scope("s_lower"):
-                    lower_panels(aug)
-
-        @pl.when(q == 3)
-        def _():
-            fin[3, 32 * i:32 * i + 32, :] = hdot(w[32 * i:32 * i + 32, :], left[...])
-            send_piece(3, i)
 
     def turn(q, carry):
         with jax.named_scope("i_base"):
-            base(at, w, sub, lane, lambda i: hook(q, i))
+            base(at, w, sub, lane, lambda i: early_hook(q, i))
 
         @pl.when(q == 0)
         def _():
@@ -375,24 +392,27 @@
             with jax.named_scope("k_second"):
                 second_block(w, lf, lr, u01, at, ridge)
 
-        @pl.when(q == 1)
-        def _():
-            w1[...] = w[...]
-            with jax.named_scope("l_chunk23"):
-                for s in range(2, 4):
-                    to_partner(s).wait_recv()
-                    load_chunk(s, g, lf, lr)
-            with jax.named_scope("l_third"):
-                third_block(w0, w1, u01, lf, lr, aug, at, ridge)
-
-        @pl.when(q == 2)
-        def _():
-            with jax.named_scope("m_last"):
-                last_panel(w, aug, at, left, fin)
-            for i in range(4):
-                send_piece(2, i)
-
         return carry
+
+    def third_hook(i):
+        if i == 1:
+            for e in range(2):
+                for n in range(4):
+                    send_piece(e, n)
+            to_partner(3).wait_recv()
+            load_chunk(3, g, lf, lr)
+            lower_panels(w0, w1, u01, lf, lr, xf, xr, aug, ridge, first_col)
+
+    def finish(n):
+        rows = slice(32 * n, 32 * n + 32)
+        fin[3, rows, :] = hdot(w[rows, :], left[...])
+
+    def last_hook(i):
+        if i > 0:
+            send_piece(3, i - 1)
+        finish(i)
+        if i == 3:
+            send_piece(3, 3)
 
     with jax.named_scope("g_half"):
         half[0] = half_block(g, core)
@@ -404,7 +424,24 @@
     with jax.named_scope("h_swap"):
         swap().wait_recv()
     at[...] = ridged(half[0] + half[1], 0, 0, ridge)
-    lax.fori_loop(0, 4, turn, 0)
+    lax.fori_loop(0, 2, turn, 0)
+    w1[...] = w[...]
+    with jax.named_scope("l_chunk2"):
+        to_partner(2).wait_recv()
+        load_chunk(2, g, lf, lr)
+    with jax.named_scope("l_third"):
+        third_block(w0, w1, u01, lf, lr, aug, at, ridge)
+    with jax.named_scope("l_arrived"):
+        arrived()
+    with jax.named_scope("l_base2"):
+        upper_strip(w0, w1, u01, lf, lr, xf, xr, aug, fin, ridge, first_col)
+        base(at, w, sub, lane, third_hook)
+    with jax.named_scope("m_last"):
+        last_panel(w, aug, at, left, fin)
+    for n in range(4):
+        send_piece(2, n)
+    with jax.named_scope("m_base3"):
+        base(at, w, sub, lane, last_hook)
 
     with jax.named_scope("n_final"):
         bulk(fin.at[:, 0:112, :], r6.at[0]).wait_recv()

time: 53.4 us -> 56.2 us (1.052)
  the two profiles are of different devices: /device:TPU:1 before, /device:TPU:97 now
where the time goes in v6:
time: 56.2 us; the launch traced here: 56.1 us
  Pallas kernels  54.5 us (97%)
  other arithmetic  0.92 us (2%)
  between operations  0.67 us (1%)
    pallas_call x1, Pallas kernels, local(): pl.pallas_call(kernel, out_shape=pltpu.VMEM((2, 32, 2048), F32), in_specs...  54.5 us

profile of v6, /device:TPU:97, one launch (start us, length us, event | category | flops | bytes accessed | tf_op | source)
XLA Modules:
  0.0 56.1 jit_solution(2489617726362399766)
XLA Ops:
  0.7 54.5 %shard_map.37 = f32[2,32,2048]{2,1,0:T(8,128)S(1)} custom-call(bf16[128,2048]{1,0:T(8,128)(2,1)} %pre.1, bf16[2048,128]{1,0:T(8,128)(2,1)} %res.1, f32[1]{0:T(128)S(6)} %copy.4.rd), custom_call_target="tpu_custom_call" | custom-call | tf_op jit(solution)/shard_map/pallas_call | solution.py:468
  55.2 0.9 %fusion = f32[2,32,2048]{2,1,0:T(8,128)} fusion(f32[2,32,2048]{2,1,0:T(8,128)S(1)} %shard_map.37, s32[]{:T(128)S(6)} %mul.16, s32[2]{0:T(128)S(1)} %iota_multiply_fusion, s32[2048]{0:T(1024)S(1)} %iota_add_fusion), kind=kLoop, calls=%fused_computation.1 | loop fusion | flops 524288 | bytes 1056780 | tf_op jit(solution)/shard_map/jit(_where)/select_n | solution.py:500
  (2 shorter events, 0.0 us)

commit v7 on v6

--- a/solution.py
+++ b/solution.py
@@ -294,14 +294,7 @@
         for d in offsets:
             kind(d).start()
 
-    @pl.when(zhi != 0)
-    def _():
-        move(move_cols, range(1, 8))
-        move(move_rows, range(1, 8))
-
-    @pl.when(zhi == 0)
-    def _():
-        move(move_cols, (1, 7))
+    move(move_cols, (1, 7))
 
     def forward_ring(q):
         @pl.when(zhi == 0)
@@ -341,22 +334,13 @@
 
     with jax.named_scope("b_ring0"):
         forward_ring(0)
-
-    @pl.when(zhi == 0)
-    def _():
-        move(move_cols, (2, 6, 4))
-
+    with jax.named_scope("b_ring123"):
+        for q in range(1, 4):
+            forward_ring(q)
+    move(move_cols, range(2, 7))
+    move(move_rows, range(1, 8))
     with jax.named_scope("c_plane0"):
         forward_plane(0)
-    with jax.named_scope("d_ring123"):
-        for q in range(1, 4):
-            forward_ring(q)
-
-    @pl.when(zhi == 0)
-    def _():
-        move(move_cols, (3, 5))
-        move(move_rows, range(1, 8))
-
     with jax.named_scope("e_plane1"):
         forward_plane(1)
     with jax.named_scope("f_gathered0"):

time: 56.2 us -> 50.2 us (0.89)
  the two profiles are of different devices: /device:TPU:97 before, /device:TPU:1 now
where the time goes in v7:
time: 50.2 us; the launch traced here: 50.1 us
  Pallas kernels  48.5 us (97%)
  other arithmetic  0.92 us (2%)
  between operations  0.67 us (1%)
    pallas_call x1, Pallas kernels, local(): pl.pallas_call(kernel, out_shape=pltpu.VMEM((2, 32, 2048), F32), in_specs...  48.5 us

profile of v7, /device:TPU:1, one launch (start us, length us, event | category | flops | bytes accessed | tf_op | source)
XLA Modules:
  0.0 50.1 jit_solution(11272179800386871852)
XLA Ops:
  0.7 48.5 %shard_map.37 = f32[2,32,2048]{2,1,0:T(8,128)S(1)} custom-call(bf16[128,2048]{1,0:T(8,128)(2,1)} %pre.1, bf16[2048,128]{1,0:T(8,128)(2,1)} %res.1, f32[1]{0:T(128)S(6)} %copy.4.rd), custom_call_target="tpu_custom_call" | custom-call | tf_op jit(solution)/shard_map/pallas_call | solution.py:452
  49.2 0.9 %fusion = f32[2,32,2048]{2,1,0:T(8,128)} fusion(f32[2,32,2048]{2,1,0:T(8,128)S(1)} %shard_map.37, s32[]{:T(128)S(6)} %mul.16, s32[2]{0:T(128)S(1)} %iota_multiply_fusion, s32[2048]{0:T(1024)S(1)} %iota_add_fusion), kind=kLoop, calls=%fused_computation.1 | loop fusion | flops 524288 | bytes 1056780 | tf_op jit(solution)/shard_map/jit(_where)/select_n | solution.py:484
  (2 shorter events, 0.0 us)

commit v8 on v7

--- a/solution.py
+++ b/solution.py
@@ -139,16 +139,29 @@
     return x0, x1
 
 
-def strip(rows, lf, lr, xf, xr, aug, ridge, first_col):
-    part = bdot(lf[rows, :], jnp.maximum(xf[...], 0)) * (1.0 / 1024) - bdot(lr[rows, :], xr[...], 1, 1)
-    aug[rows, 256:512] = ridged(part, rows.start, first_col, ridge)
-
-
-def upper_strip(w0, w, u01, lf, lr, xf, xr, aug, fin, ridge, first_col):
-    strip(slice(0, 256), lf, lr, xf, xr, aug, ridge, first_col)
-    x0, x1 = first_panels(slice(256, 512), w0, w, u01, aug)
-    fin[0] = x0
-    fin[1] = x1
+def half_cols(h):
+    return slice(256 + 128 * h, 384 + 128 * h)
+
+
+def strip(h, rows, lf, lr, xf, xr, aug, ridge, first_col):
+    cut = slice(128 * h, 128 * h + 128)
+    part = bdot(lf[rows, :], jnp.maximum(xf[:, cut], 0)) * (1.0 / 1024) - bdot(lr[rows, :], xr[cut, :], 1, 1)
+    aug[rows, half_cols(h)] = ridged(part, rows.start, first_col + 128 * h, ridge)
+
+
+def first_row(h, w0, u01, aug, fin):
+    cols = half_cols(h)
+    x0 = hdot(w0[...], aug[0:128, cols])
+    aug[0:128, cols] = x0
+    fin[0, :, 128 * h:128 * h + 128] = x0
+    aug[128:256, cols] = aug[128:256, cols] - hdot(u01[...], x0, 0, 0)
+
+
+def second_row(h, w, aug, fin):
+    cols = half_cols(h)
+    x1 = hdot(w[...], aug[128:256, cols])
+    aug[128:256, cols] = x1
+    fin[1, :, 128 * h:128 * h + 128] = x1
 
 
 def third_block(w0, w, u01, lf, lr, aug, at, ridge):
@@ -159,13 +172,15 @@
     at[...] = aug[256:384, cols] - hdot(left, left, 0, 0)
 
 
-def lower_panels(w0, w, u01, lf, lr, xf, xr, aug, ridge, first_col):
+def last_column(w0, w, u01, lf, lr, aug, ridge):
     cols = slice(128, 256)
     aug[:, cols] = ridged(gram(lf, lr, slice(0, 512), slice(384, 512)), 0, 384, ridge)
     first_panels(cols, w0, w, u01, aug)
-    strip(slice(256, 512), lf, lr, xf, xr, aug, ridge, first_col)
-    aug[256:384, 128:512] = aug[256:384, 128:512] - hdot(aug[0:256, 0:128], aug[0:256, 128:512], 0, 0)
-    aug[384:512, 128:512] = aug[384:512, 128:512] - hdot(aug[0:256, 128:256], aug[0:256, 128:512], 0, 0)
+
+
+def lower_panels(cols, aug):
+    aug[256:384, cols] = aug[256:384, cols] - hdot(aug[0:256, 0:128], aug[0:256, cols], 0, 0)
+    aug[384:512, cols] = aug[384:512, cols] - hdot(aug[0:256, 128:256], aug[0:256, cols], 0, 0)
 
 
 def last_panel(w, aug, at, left, fin):
@@ -244,21 +259,28 @@
 
     root = (spot == 0) & (zhi == 0)
 
-    def block_of(to):
-        return pl.ds(pl.multiple_of(256 * to, 256), 256)
-
     home = pl.ds(pl.multiple_of(128 * col, 128), 128)
 
-    def move_cols(d):
+    def part_of(to, h):
+        return pl.ds(pl.multiple_of(256 * to + 128 * h, 128), 128)
+
+    def halves(h):
+        cut = slice(128 * h, 128 * h + 128)
+        return xf.at[home, cut], xr.at[cut, home]
+
+    def move_cols(h, d):
         to = lax.rem(col + d, 8)
-        return remote(pre.at[:, block_of(to)], xf.at[home, :], sent.at[4], r5.at[0], row, to)
-
-    def move_rows(d):
+        return remote(pre.at[:, part_of(to, h)], halves(h)[0], sent.at[4], r5.at[2 * h], row, to)
+
+    def move_rows(h, d):
         to = lax.rem(col + d, 8)
-        return remote(res.at[block_of(to), :], xr.at[:, home], sent.at[5], r5.at[1], row, to)
-
-    keep_cols = pltpu.make_async_copy(pre.at[:, block_of(col)], xf.at[home, :], loc.at[0])
-    keep_rows = pltpu.make_async_copy(res.at[block_of(col), :], xr.at[:, home], loc.at[1])
+        return remote(res.at[part_of(to, h), :], halves(h)[1], sent.at[5], r5.at[2 * h + 1], row, to)
+
+    def stay(h):
+        return (
+            pltpu.make_async_copy(pre.at[:, part_of(col, h)], halves(h)[0], loc.at[2 * h]),
+            pltpu.make_async_copy(res.at[part_of(col, h), :], halves(h)[1], loc.at[2 * h + 1]),
+        )
 
     here = pl.ds(pl.multiple_of(256 * col, 256), 256)
 
@@ -267,7 +289,7 @@
         return remote(fin.at[q, 32 * i:32 * i + 32, :], out.at[q // 2, :, here], sent.at[6], r6.at[0], row, to)
 
     def keep(q, i):
-        return pltpu.make_async_copy(fin.at[q, 32 * i:32 * i + 32, :], out.at[q // 2, :, here], loc.at[2])
+        return pltpu.make_async_copy(fin.at[q, 32 * i:32 * i + 32, :], out.at[q // 2, :, here], loc.at[4])
 
     def send_piece(q, i):
         to = 4 * (q % 2) + i
@@ -279,6 +301,22 @@
         @pl.when(col != to)
         def _():
             deliver(q, i).start()
+
+    def send_half(q, h):
+        cut = slice(128 * h, 128 * h + 128)
+        lanes = pl.ds(pl.multiple_of(256 * col + 128 * h, 128), 128)
+        for i in range(4):
+            to = 4 * (q % 2) + i
+            src = fin.at[q, 32 * i:32 * i + 32, cut]
+            dst = out.at[q // 2, :, lanes]
+
+            @pl.when(col == to)
+            def _():
+                pltpu.make_async_copy(src, dst, loc.at[4]).start()
+
+            @pl.when(col != to)
+            def _():
+                remote(src, dst, sent.at[6], r6.at[0], row, to).start()
 
     @pl.when(root)
     def _():
@@ -287,14 +325,22 @@
             for p in range(1, 16):
                 scatter(q, p).start()
 
-    keep_cols.start()
-    keep_rows.start()
-
-    def move(kind, offsets):
+    for h in range(2):
+        for copy in stay(h):
+            copy.start()
+
+    def move(kind, h, offsets):
         for d in offsets:
-            kind(d).start()
-
-    move(move_cols, (1, 7))
+            kind(h, d).start()
+
+    @pl.when(zhi != 0)
+    def _():
+        move(move_cols, 0, range(1, 8))
+        move(move_rows, 0, range(1, 8))
+
+    @pl.when(zhi == 0)
+    def _():
+        move(move_cols, 0, (1, 7, 2, 6))
 
     def forward_ring(q):
         @pl.when(zhi == 0)
@@ -337,8 +383,12 @@
     with jax.named_scope("b_ring123"):
         for q in range(1, 4):
             forward_ring(q)
-    move(move_cols, range(2, 7))
-    move(move_rows, range(1, 8))
+
+    @pl.when(zhi == 0)
+    def _():
+        move(move_cols, 0, (3, 4, 5))
+        move(move_rows, 0, range(1, 8))
+
     with jax.named_scope("c_plane0"):
         forward_plane(0)
     with jax.named_scope("e_plane1"):
@@ -346,46 +396,37 @@
     with jax.named_scope("f_gathered0"):
         gathered(0)
 
-    def arrived():
-        keep_cols.wait()
-        keep_rows.wait()
-        bulk(xf.at[0:896, :], r5.at[0]).wait_recv()
-        bulk(xr.at[:, 0:896], r5.at[1]).wait_recv()
-
-    def early_hook(q, i):
+    def arrived(h):
+        for copy in stay(h):
+            copy.wait()
+        bulk(xf.at[0:896, 0:128], r5.at[2 * h]).wait_recv()
+        bulk(xr.at[0:128, 0:896], r5.at[2 * h + 1]).wait_recv()
+
+    def first_hook(i):
         if i == 1:
-            with jax.named_scope("j_share"):
-                share(q + 1)
+            share(1)
+
+    def second_hook(i):
+        if i == 0:
+            share(2)
         if i == 2:
-            @pl.when(q == 1)
-            def _():
-                with jax.named_scope("j_share3"):
-                    share(3)
-
-    def turn(q, carry):
-        with jax.named_scope("i_base"):
-            base(at, w, sub, lane, lambda i: early_hook(q, i))
-
-        @pl.when(q == 0)
-        def _():
-            w0[...] = w[...]
-            with jax.named_scope("k_chunk01"):
-                for s in range(2):
-                    to_partner(s).wait_recv()
-                    load_chunk(s, g, lf, lr)
-            with jax.named_scope("k_second"):
-                second_block(w, lf, lr, u01, at, ridge)
-
-        return carry
+            share(3)
 
     def third_hook(i):
+        if i == 0:
+            arrived(1)
+            strip(1, slice(0, 256), lf, lr, xf, xr, aug, ridge, first_col)
+            first_row(1, w0, u01, aug, fin)
+            second_row(1, w1, aug, fin)
         if i == 1:
-            for e in range(2):
-                for n in range(4):
-                    send_piece(e, n)
+            send_half(1, 1)
+            send_half(0, 1)
             to_partner(3).wait_recv()
             load_chunk(3, g, lf, lr)
-            lower_panels(w0, w1, u01, lf, lr, xf, xr, aug, ridge, first_col)
+            last_column(w0, w1, u01, lf, lr, aug, ridge)
+            strip(0, slice(256, 512), lf, lr, xf, xr, aug, ridge, first_col)
+            strip(1, slice(256, 512), lf, lr, xf, xr, aug, ridge, first_col)
+            lower_panels(slice(128, 512), aug)
 
     def finish(n):
         rows = slice(32 * n, 32 * n + 32)
@@ -405,20 +446,37 @@
     with jax.named_scope("g_plane23"):
         forward_plane(2)
         forward_plane(3)
+    move(move_cols, 1, range(1, 8))
+    move(move_rows, 1, range(1, 8))
     with jax.named_scope("h_swap"):
         swap().wait_recv()
     at[...] = ridged(half[0] + half[1], 0, 0, ridge)
-    lax.fori_loop(0, 2, turn, 0)
+    with jax.named_scope("i_base0"):
+        base(at, w, sub, lane, first_hook)
+    w0[...] = w[...]
+    with jax.named_scope("k_chunk01"):
+        for s in range(2):
+            to_partner(s).wait_recv()
+            load_chunk(s, g, lf, lr)
+    with jax.named_scope("k_second"):
+        second_block(w, lf, lr, u01, at, ridge)
+    with jax.named_scope("k_arrived"):
+        arrived(0)
+    with jax.named_scope("k_base1"):
+        strip(0, slice(0, 256), lf, lr, xf, xr, aug, ridge, first_col)
+        first_row(0, w0, u01, aug, fin)
+        base(at, w, sub, lane, second_hook)
     w1[...] = w[...]
+    second_row(0, w, aug, fin)
+    send_half(1, 0)
+    send_half(0, 0)
+    with jax.named_scope("l_partner2"):
+        to_partner(2).wait_recv()
     with jax.named_scope("l_chunk2"):
-        to_partner(2).wait_recv()
         load_chunk(2, g, lf, lr)
     with jax.named_scope("l_third"):
         third_block(w0, w1, u01, lf, lr, aug, at, ridge)
-    with jax.named_scope("l_arrived"):
-        arrived()
     with jax.named_scope("l_base2"):
-        upper_strip(w0, w1, u01, lf, lr, xf, xr, aug, fin, ridge, first_col)
         base(at, w, sub, lane, third_hook)
     with jax.named_scope("m_last"):
         last_panel(w, aug, at, left, fin)
@@ -430,7 +488,7 @@
     with jax.named_scope("n_final"):
         bulk(fin.at[:, 0:112, :], r6.at[0]).wait_recv()
     with jax.named_scope("o_sends"):
-        pltpu.make_async_copy(fin.at[0, 0:64, :], fin.at[1, 0:64, :], loc.at[2]).wait()
+        pltpu.make_async_copy(fin.at[0, 0:64, :], fin.at[1, 0:64, :], loc.at[4]).wait()
         bulk(fin.at[:, 0:112, :], sent.at[6]).wait_send()
         bulk(xf.at[0:896, :], sent.at[4]).wait_send()
         bulk(xr.at[:, 0:896], sent.at[5]).wait_send()
@@ -473,9 +531,9 @@
             pltpu.VMEM((128, 128), F32),
             pltpu.VMEM((128, 128), F32),
             pltpu.VMEM((4, 128, 256), F32),
-            dma((3,)), dma((7,)),
+            dma((5,)), dma((7,)),
             dma((4,)), dma((4,)), dma((4,)), dma((4,)),
-            dma((2,)), dma((1,)), dma((2,)),
+            dma((4,)), dma((1,)), dma((2,)),
         ],
         compiler_params=pltpu.CompilerParams(collective_id=0, has_side_effects=True),
     )(preacts, resident, ridge)

time: 50.2 us -> 49.1 us (0.978); the launches traced: 50.1 us -> 48.2 us
  Pallas kernels: 48.5 us -> 46.6 us
    pallas_call x1, Pallas kernels: 48.5 us -> 46.6 us  [local(): pl.pallas_call(kernel, out_shape=pltpu.VMEM((2, 32, 2048), F32), in_specs...]
where the time goes in v8:
time: 49.1 us; the launch traced here: 48.2 us
  Pallas kernels  46.6 us (95%)
  other arithmetic  0.92 us (2%)
  between operations  0.67 us (1%)
    pallas_call x1, Pallas kernels, local(): pl.pallas_call(kernel, out_shape=pltpu.VMEM((2, 32, 2048), F32), in_specs...  46.6 us

profile of v8, /device:TPU:1, one launch (start us, length us, event | category | flops | bytes accessed | tf_op | source)
XLA Modules:
  0.0 48.2 jit_solution(13167119354345220649)
XLA Ops:
  0.7 46.6 %shard_map.37 = f32[2,32,2048]{2,1,0:T(8,128)S(1)} custom-call(bf16[128,2048]{1,0:T(8,128)(2,1)} %pre.1, bf16[2048,128]{1,0:T(8,128)(2,1)} %res.1, f32[1]{0:T(128)S(6)} %copy.4.rd), custom_call_target="tpu_custom_call" | custom-call | tf_op jit(solution)/shard_map/pallas_call | solution.py:510
  47.3 0.9 %fusion = f32[2,32,2048]{2,1,0:T(8,128)} fusion(f32[2,32,2048]{2,1,0:T(8,128)S(1)} %shard_map.37, s32[]{:T(128)S(6)} %mul.16, s32[2]{0:T(128)S(1)} %iota_multiply_fusion, s32[2048]{0:T(1024)S(1)} %iota_add_fusion), kind=kLoop, calls=%fused_computation.1 | loop fusion | flops 524288 | bytes 1056780 | tf_op jit(solution)/shard_map/jit(_where)/select_n | solution.py:542
  (2 shorter events, 0.0 us)

commit v9 on v8

--- a/solution.py
+++ b/solution.py
@@ -421,9 +421,6 @@
         if i == 1:
             send_half(1, 1)
             send_half(0, 1)
-            to_partner(3).wait_recv()
-            load_chunk(3, g, lf, lr)
-            last_column(w0, w1, u01, lf, lr, aug, ridge)
             strip(0, slice(256, 512), lf, lr, xf, xr, aug, ridge, first_col)
             strip(1, slice(256, 512), lf, lr, xf, xr, aug, ridge, first_col)
             lower_panels(slice(128, 512), aug)
@@ -433,11 +430,11 @@
         fin[3, rows, :] = hdot(w[rows, :], left[...])
 
     def last_hook(i):
-        if i > 0:
+        if i > 1:
             send_piece(3, i - 1)
         finish(i)
-        if i == 3:
-            send_piece(3, 3)
+        if i in (0, 3):
+            send_piece(3, i)
 
     with jax.named_scope("g_half"):
         half[0] = half_block(g, core)
@@ -476,7 +473,11 @@
         load_chunk(2, g, lf, lr)
     with jax.named_scope("l_third"):
         third_block(w0, w1, u01, lf, lr, aug, at, ridge)
+    with jax.named_scope("l_partner3"):
+        to_partner(3).wait_recv()
     with jax.named_scope("l_base2"):
+        load_chunk(3, g, lf, lr)
+        last_column(w0, w1, u01, lf, lr, aug, ridge)
         base(at, w, sub, lane, third_hook)
     with jax.named_scope("m_last"):
         last_panel(w, aug, at, left, fin)

time: 49.1 us -> 48.8 us (level)
  no operation moved by 1% of the time
where the time goes in v9:
time: 48.8 us; the launch traced here: 48.2 us
  Pallas kernels  46.6 us (95%)
  other arithmetic  0.92 us (2%)
  between operations  0.67 us (1%)
    pallas_call x1, Pallas kernels, local(): pl.pallas_call(kernel, out_shape=pltpu.VMEM((2, 32, 2048), F32), in_specs...  46.6 us

profile of v9, /device:TPU:1, one launch (start us, length us, event | category | flops | bytes accessed | tf_op | source)
XLA Modules:
  0.0 48.2 jit_solution(861341675184049569)
XLA Ops:
  0.7 46.6 %shard_map.37 = f32[2,32,2048]{2,1,0:T(8,128)S(1)} custom-call(bf16[128,2048]{1,0:T(8,128)(2,1)} %pre.1, bf16[2048,128]{1,0:T(8,128)(2,1)} %res.1, f32[1]{0:T(128)S(6)} %copy.4.rd), custom_call_target="tpu_custom_call" | custom-call | tf_op jit(solution)/shard_map/pallas_call | solution.py:511
  47.3 0.9 %fusion = f32[2,32,2048]{2,1,0:T(8,128)} fusion(f32[2,32,2048]{2,1,0:T(8,128)S(1)} %shard_map.37, s32[]{:T(128)S(6)} %mul.16, s32[2]{0:T(128)S(1)} %iota_multiply_fusion, s32[2048]{0:T(1024)S(1)} %iota_add_fusion), kind=kLoop, calls=%fused_computation.1 | loop fusion | flops 524288 | bytes 1056780 | tf_op jit(solution)/shard_map/jit(_where)/select_n | solution.py:543
  (2 shorter events, 0.0 us)

commit v10 on v9

--- a/solution.py
+++ b/solution.py
@@ -421,7 +421,6 @@
         if i == 1:
             send_half(1, 1)
             send_half(0, 1)
-            strip(0, slice(256, 512), lf, lr, xf, xr, aug, ridge, first_col)
             strip(1, slice(256, 512), lf, lr, xf, xr, aug, ridge, first_col)
             lower_panels(slice(128, 512), aug)
 
@@ -478,6 +477,7 @@
     with jax.named_scope("l_base2"):
         load_chunk(3, g, lf, lr)
         last_column(w0, w1, u01, lf, lr, aug, ridge)
+        strip(0, slice(256, 512), lf, lr, xf, xr, aug, ridge, first_col)
         base(at, w, sub, lane, third_hook)
     with jax.named_scope("m_last"):
         last_panel(w, aug, at, left, fin)

time: 48.8 us -> 48.6 us (level); the launches traced: 48.2 us -> 48.5 us
  no operation moved by 1% of the time
where the time goes in v10:
time: 48.6 us; the launch traced here: 48.5 us
  Pallas kernels  46.9 us (97%)
  other arithmetic  0.92 us (2%)
  between operations  0.67 us (1%)
    pallas_call x1, Pallas kernels, local(): pl.pallas_call(kernel, out_shape=pltpu.VMEM((2, 32, 2048), F32), in_specs...  46.9 us

profile of v10, /device:TPU:1, one launch (start us, length us, event | category | flops | bytes accessed | tf_op | source)
XLA Modules:
  0.0 48.5 jit_solution(14237183608403796942)
XLA Ops:
  0.7 46.9 %shard_map.37 = f32[2,32,2048]{2,1,0:T(8,128)S(1)} custom-call(bf16[128,2048]{1,0:T(8,128)(2,1)} %pre.1, bf16[2048,128]{1,0:T(8,128)(2,1)} %res.1, f32[1]{0:T(128)S(6)} %copy.4.rd), custom_call_target="tpu_custom_call" | custom-call | tf_op jit(solution)/shard_map/pallas_call | solution.py:511
  47.6 0.9 %fusion = f32[2,32,2048]{2,1,0:T(8,128)} fusion(f32[2,32,2048]{2,1,0:T(8,128)S(1)} %shard_map.37, s32[]{:T(128)S(6)} %mul.16, s32[2]{0:T(128)S(1)} %iota_multiply_fusion, s32[2048]{0:T(1024)S(1)} %iota_add_fusion), kind=kLoop, calls=%fused_computation.1 | loop fusion | flops 524288 | bytes 1056780 | tf_op jit(solution)/shard_map/jit(_where)/select_n | solution.py:543
  (2 shorter events, 0.0 us)
